TPU v7x, 32 devices: a whole 2x2x4 slice. The times are simulated.
32 devices in a mesh: frames: 8 (over z, y), rows: 4 (over x, core).
Axes of the slice: x: 2, y: 2, z: 4, core: 2. Of those that a mesh axis runs over, the one named last changes fastest.
Arguments:
- features: bfloat16 [8, 64, 128, 128], P('frames', 'rows'), may hold values from -6 to 6
- pair_weight: bfloat16 [8, 64, 4, 128, 128], P('frames', 'rows'), may hold values from -0.5 to 0.5
- target_tile: int32 [8, 64, 4], P('frames', 'rows'), may hold values from 0 to 31, all different within a row; in each aligned block of 16 rows (0 to 15, 16 to 31, ..., all dimensions but the last counted through in order) at most 4 rows name the same one
- target_block: int32 [8, 64, 4], P('frames', 'rows'), may hold values from 0 to 15
- conv1_weight: bfloat16 [3, 3, 3, 128, 128], replicated, may hold values from -0.109375 to 0.109375
- conv1_bias: float32 [128], replicated, may hold values from -3 to 3
- conv2_weight: bfloat16 [3, 3, 3, 128, 128], replicated, may hold values from -0.109375 to 0.109375
- conv2_bias: float32 [128], replicated, may hold values from -3 to 3
Outputs:
- occupancy: bfloat16 [64, 256, 4, 128], P('frames', 'rows')
Inputs may be any that keep to these rules, and one draw needn't show every extreme that they name: `target_tile`: each image block names 4 different tiles; among the pairs of one device no tile is named more than 4 times, a bound that some block reaches.
All inputs are finite; a program needn't handle non-finite values.
Results may differ from a plain program's by a relative error of at most 0.0055.
Values may be sent and summed in bfloat16 or wider, within the bound.
No kernel may reach another device: no remote copies, remote signals or barrier semaphores. Data moves between devices by JAX's collectives and lax.ppermute only.
A program may use at most 128 MiB of HBM per device.

v0:
```python
import functools

import jax
import jax.numpy as jnp
from jax import lax
from jax.experimental import pallas as pl
from jax.experimental.pallas import tpu as pltpu
from jax.sharding import PartitionSpec as P

DEPTH = 4
TX = 8
TY = 64
LABEL_ROWS = 16
VMEM = pltpu.VMEM
LIMIT = 60 * 1024 * 1024


def vmem():
    return pl.BlockSpec(memory_space=pltpu.VMEM)


def smem():
    return pl.BlockSpec(memory_space=pltpu.SMEM)


def contribute_kernel(tiles, capacity, top, tile_ref, block_ref, weight_ref, feature_ref, out_ref, counts, labels):
    images = feature_ref.shape[0]
    size = feature_ref.shape[1]

    def clear(t, carry):
        counts[t] = 0
        for k in range(capacity):
            labels[t * capacity + k] = -1
        return carry

    lax.fori_loop(0, tiles, clear, 0)

    def image(b, carry):
        weights = weight_ref[b].reshape(top * size, size)
        product = jnp.dot(weights, feature_ref[b], preferred_element_type=jnp.float32)
        product = product.astype(jnp.bfloat16)
        for t in range(top):
            tile = tile_ref[b * top + t]
            rank = counts[tile]
            counts[tile] = rank + 1
            labels[tile * capacity + rank] = block_ref[b * top + t]
            out_ref[tile, pl.ds(pl.multiple_of(rank * size, size), size), :] = product[t * size : (t + 1) * size]
        return carry

    lax.fori_loop(0, images, image, 0)
    lane = lax.broadcasted_iota(jnp.int32, (LABEL_ROWS, out_ref.shape[2]), 1)

    def mark(t, carry):
        row = jnp.full(lane.shape, -1, jnp.int32)
        for k in range(capacity):
            row = jnp.where(lane == k, labels[t * capacity + k], row)
        out_ref[t, capacity * size :, :] = row.astype(jnp.float32).astype(jnp.bfloat16)
        return carry

    lax.fori_loop(0, tiles, mark, 0)


def gather_kernel(tiles, capacity, size, received_ref, out_ref, total, marks, marks_smem, sem):
    base = capacity * size

    def read(t, carry):
        row = received_ref[t, base : base + LABEL_ROWS, :].astype(jnp.float32)
        marks[pl.ds(t, 1), :] = row[0:1, :].astype(jnp.int32)
        return carry

    lax.fori_loop(0, tiles, read, 0)
    copy = pltpu.make_async_copy(marks, marks_smem, sem)
    copy.start()
    total[...] = jnp.zeros_like(total)
    copy.wait()

    def add(t, carry):
        for k in range(capacity):
            label = marks_smem[t, k]

            @pl.when(label >= 0)
            def _():
                rows = pl.ds(pl.multiple_of(label * size, size), size)
                total[rows, :] += received_ref[t, k * size : (k + 1) * size, :].astype(jnp.float32)

        return carry

    lax.fori_loop(0, tiles, add, 0)
    cells = total.shape[0] // DEPTH
    channels = total.shape[1]
    for z in range(DEPTH):
        part = total[pl.ds(z, cells, stride=DEPTH), :]
        out_ref[:, z * channels : (z + 1) * channels] = part.astype(jnp.bfloat16)


def band_kernel(first_ref, second_ref, out1_ref, out2_ref):
    channels = first_ref.shape[-1]
    zero = jnp.zeros((channels, channels), jnp.bfloat16)
    for source, target in ((first_ref, out1_ref), (second_ref, out2_ref)):
        for dx in range(3):
            for half in range(2):
                for dy in range(3):
                    for k in range(3):
                        z_in = k + half
                        for j in range(2):
                            dz = z_in - (2 * half + j) + 1
                            value = source[dx, dy, dz] if 0 <= dz < 3 else zero
                            row = (dy * 3 + k) * channels
                            target[dx, half, row : row + channels, j * channels : (j + 1) * channels] = value


def convolve_half(copies, bands, half, out_rows, channels):
    total = None
    for dx in range(3):
        pieces = []
        for dy in range(3):
            piece = copies[dy][dx : dx + out_rows, :, half * channels : (half + 3) * channels]
            pieces.append(piece.reshape(-1, 3 * channels))
        product = jnp.dot(
            jnp.concatenate(pieces, axis=1), bands[dx, half], preferred_element_type=jnp.float32
        )
        total = product if total is None else total + product
    return total


def silu(v):
    return v / (1.0 + jnp.exp(-v))


def convolve_kernel(
    ends_ref, main_ref, low_ref, high_ref, left_ref, right_ref,
    band1_ref, band2_ref, bias1_ref, bias2_ref, out_ref,
    copies0, copies1, copies2, hidden, shift1, shift2, stage,
):
    channels = bias1_ref.shape[1]
    rows, cols = main_ref.shape[0], main_ref.shape[1]
    for x0, source in ((0, low_ref), (2, main_ref), (2 + rows, high_ref)):
        value = source[...]
        part = slice(x0, x0 + value.shape[0])
        copies0[part, 2 : 2 + cols, :] = value
        copies1[part, 1 : 1 + cols, :] = value
        copies2[part, 0:cols, :] = value
    left = left_ref[...]
    right = right_ref[...]
    copies0[:, 0:2, :] = left
    copies1[:, 0:1, :] = left[:, 1:2]
    copies1[:, 1 + cols : 2 + cols, :] = right[:, 0:1]
    copies2[:, cols : 2 + cols, :] = right
    for half in range(2):
        total = convolve_half((copies0, copies1, copies2), band1_ref, half, rows + 2, channels)
        bias = jnp.concatenate([bias1_ref[...], bias1_ref[...]], axis=1)
        value = silu(total + bias).reshape(rows + 2, -1, 2 * channels)
        x_at = lax.broadcasted_iota(jnp.int32, value.shape, 0)
        y_at = lax.broadcasted_iota(jnp.int32, value.shape, 1)
        keep = (x_at >= ends_ref[0]) & (x_at < rows + 2 - ends_ref[1])
        keep = keep & (y_at >= ends_ref[2]) & (y_at < cols + 2 - ends_ref[3])
        value = jnp.where(keep, value, 0.0).astype(jnp.bfloat16)
        hidden[:, :, half * 2 * channels : (half + 1) * 2 * channels] = value
    shift1[...] = hidden[:, 1 : 1 + cols, :]
    shift2[...] = hidden[:, 2 : 2 + cols, :]
    for half in range(2):
        total = convolve_half(
            (hidden.at[:, 0:cols, :], shift1, shift2), band2_ref, half, rows, channels
        )
        for j in range(2):
            value = silu(total[:, j * channels : (j + 1) * channels] + bias2_ref[...])
            stage[pl.ds(2 * half + j, rows * cols, stride=DEPTH), :] = value
    out_ref[...] = stage[...].astype(jnp.bfloat16)


def shards(features, pair_weight, target_tile, target_block, conv1_weight, conv1_bias, conv2_weight, conv2_bias):
    images, size, channels = features.shape[1:]
    top = target_tile.shape[2]
    n_frames = lax.axis_size("frames")
    n_rows = lax.axis_size("rows")
    devices = n_frames * n_rows
    capacity = max(2, 2 * images * top // devices)
    message = capacity * size + LABEL_ROWS
    params = pltpu.CompilerParams(vmem_limit_bytes=LIMIT)
    outgoing = pl.pallas_call(
        functools.partial(contribute_kernel, devices, capacity, top),
        out_shape=jax.ShapeDtypeStruct((devices, message, channels), jnp.bfloat16),
        in_specs=[smem(), smem(), vmem(), vmem()],
        out_specs=vmem(),
        scratch_shapes=[pltpu.SMEM((devices,), jnp.int32), pltpu.SMEM((devices * capacity,), jnp.int32)],
        compiler_params=params,
        name="contribute",
    )(target_tile.reshape(-1), target_block.reshape(-1), pair_weight[0], features[0])
    received = lax.all_to_all(outgoing, ("frames", "rows"), split_axis=0, concat_axis=0, tiled=True)
    cells = TX * TY
    grid = pl.pallas_call(
        functools.partial(gather_kernel, devices, capacity, size),
        out_shape=jax.ShapeDtypeStruct((cells, DEPTH * channels), jnp.bfloat16),
        in_specs=[vmem()],
        out_specs=vmem(),
        scratch_shapes=[
            VMEM((cells * DEPTH, channels), jnp.float32),
            VMEM((devices, channels), jnp.int32),
            pltpu.SMEM((devices, channels), jnp.int32),
            pltpu.SemaphoreType.DMA,
        ],
        compiler_params=params,
        name="gather",
    )(received)
    bands = jax.ShapeDtypeStruct((3, 2, 9 * channels, 2 * channels), jnp.bfloat16)
    band1, band2 = pl.pallas_call(
        band_kernel,
        out_shape=(bands, bands),
        in_specs=[vmem(), vmem()],
        out_specs=(vmem(), vmem()),
        compiler_params=params,
        name="bands",
    )(conv1_weight, conv2_weight)
    main = grid.reshape(TX, TY, DEPTH * channels)

    def shifted(value, axis, count, step):
        pairs = [(i, i + step) for i in range(count) if 0 <= i + step < count]
        return lax.ppermute(value, axis, pairs)

    low = shifted(main[TX - 2 :], "frames", n_frames, 1)
    high = shifted(main[:2], "frames", n_frames, -1)
    edge = jnp.concatenate([low[:, TY - 2 :], main[:, TY - 2 :], high[:, TY - 2 :]], axis=0)
    left = shifted(edge, "rows", n_rows, 1)
    edge = jnp.concatenate([low[:, :2], main[:, :2], high[:, :2]], axis=0)
    right = shifted(edge, "rows", n_rows, -1)
    f, r = lax.axis_index("frames"), lax.axis_index("rows")
    ends = jnp.stack([f == 0, f == n_frames - 1, r == 0, r == n_rows - 1]).astype(jnp.int32)
    wide = 80
    lanes = DEPTH * channels
    out = pl.pallas_call(
        convolve_kernel,
        out_shape=jax.ShapeDtypeStruct((cells * DEPTH, channels), jnp.bfloat16),
        in_specs=[smem()] + [vmem()] * 9,
        out_specs=vmem(),
        scratch_shapes=[VMEM((TX + 4, wide, lanes), jnp.bfloat16)] * 3
        + [VMEM((TX + 2, wide, lanes), jnp.bfloat16)]
        + [VMEM((TX + 2, TY, lanes), jnp.bfloat16)] * 2
        + [VMEM((cells * DEPTH, channels), jnp.float32)],
        compiler_params=params,
        name="convolve",
    )(ends, main, low, high, left, right, band1, band2, conv1_bias[None], conv2_bias[None])
    return out.reshape(TX, TY, DEPTH, channels)


def solution(mesh):
    placed = (
        P("frames", "rows", None, None),
        P("frames", "rows", None, None, None),
        P("frames", "rows", None),
        P("frames", "rows", None),
        P(),
        P(),
        P(),
        P(),
    )
    return jax.shard_map(
        shards,
        mesh=mesh,
        in_specs=placed,
        out_specs=P("frames", "rows", None, None),
        check_vma=False,
    )
```

profile of v0, /device:TPU:1, one launch (start us, length us, event | category | flops | bytes accessed | tf_op | source)
XLA Modules:
  0.0 152.4 jit_solution(14766922299861782436)
XLA Ops:
  0.0 0.8 copy.11
  0.8 0.6 reshape.14.tile_ref
  1.4 0.8 copy.12
  2.1 0.6 reshape.15.block_ref
  2.8 7.2 %contribute.1 = bf16[32,528,128]{2,1,0:T(8,128)(2,1)} custom-call(s32[64]{0:T(128)} %reshape.14.tile_ref, s32[64]{0:T(128)} %reshape.15.block_ref, bf16[16,4,128,128]{3,2,1,0:T(8,128)(2,1)} %bitcast.14, bf16[16,128,128]{2,1,0:T(8,128)(2,1)} %bitcast.15), custom_call_target="tpu_custom_call" | custom-call | tf_op jit(solution)/shard_map/contribute/pallas_call | solution.py:180
  9.9 7.1 %all-to-all-start = ((bf16[32,528,128]{2,1,0:T(8,128)(2,1)}), bf16[32,528,128]{2,1,0:T(8,128)(2,1)}, u32[]{:S(2)}, u32[]{:S(2)}) async-start(bf16[32,528,128]{2,1,0:T(8,128)(2,1)} %contribute.1), calls=%async_computation | async-start | bytes 8650752 | tf_op jit(solution)/shard_map/all_to_all | solution.py:189
  17.1 95.9 %all-to-all-done.received_ref = bf16[32,528,128]{2,1,0:T(8,128)(2,1)} async-done(((bf16[32,528,128]{2,1,0:T(8,128)(2,1)}), bf16[32,528,128]{2,1,0:T(8,128)(2,1)}, u32[]{:S(2)}, u32[]{:S(2)}) %all-to-all-start) | async-done | bytes 4325408 | tf_op jit(solution)/shard_map/all_to_all | solution.py:189
  113.0 5.6 %gather.1 = bf16[512,512]{1,0:T(8,128)(2,1)} custom-call(bf16[32,528,128]{2,1,0:T(8,128)(2,1)} %all-to-all-done.received_ref), custom_call_target="tpu_custom_call" | custom-call | tf_op jit(solution)/shard_map/gather/pallas_call | solution.py:191
  118.6 1.0 fusion.1
  119.5 3.4 %collective-permute-start = (bf16[2,64,512]{2,1,0:T(8,128)(2,1)S(1)}, bf16[2,64,512]{2,1,0:T(8,128)(2,1)S(1)}, u32[]{:S(2)}, u32[]{:S(2)}) collective-permute-start(bf16[2,64,512]{2,1,0:T(8,128)(2,1)S(1)} %bitcast.17), channel_id=1, source_target_pairs={{0,4},{4,8},{8,12},{12,16},{16,20},{20,24},{24,28},{1,5},{5,9},{9,... | collective-permute-start | bytes 393224 | tf_op jit(solution)/shard_map/ppermute | solution.py:218
  122.9 1.3 collective-permute-start.1
  124.2 0.9 fusion
  125.2 0.0 collective-permute-done.low_ref
  125.2 0.0 copy-start
  125.2 3.5 %collective-permute-done.1.high_ref = bf16[2,64,512]{2,1,0:T(8,128)(2,1)S(1)} collective-permute-done((bf16[2,64,512]{2,1,0:T(8,128)(2,1)S(1)}, bf16[2,64,512]{2,1,0:T(8,128)(2,1)S(1)}, u32[]{:S(2)}, u32[]{:S(2)}) %collective-permute-start.1) | collective-permute-done | bytes 131104 | tf_op jit(solution)/shard_map/ppermute | solution.py:218
  128.7 0.0 copy-start.1
  128.7 4.1 %collective-permute-start.3 = (bf16[12,2,512]{2,1,0:T(2,128)(2,1)S(1)}, bf16[12,2,512]{2,1,0:T(2,128)(2,1)S(1)}, u32[]{:S(2)}, u32[]{:S(2)}) collective-permute-start(bf16[12,2,512]{2,1,0:T(2,128)(2,1)S(1)} %pad_maximum_fusion.1), channel_id=1, source_target_pairs={{1,0},{2,1},{3,2},{5,4},{6,5},{7,6},{9,8},{10,9},{11,10},{13,12},{... | collective-permute-start | bytes 73736 | tf_op jit(solution)/shard_map/ppermute | solution.py:218
  132.8 3.2 %collective-permute-start.2 = (bf16[12,2,512]{2,1,0:T(2,128)(2,1)S(1)}, bf16[12,2,512]{2,1,0:T(2,128)(2,1)S(1)}, u32[]{:S(2)}, u32[]{:S(2)}) collective-permute-start(bf16[12,2,512]{2,1,0:T(2,128)(2,1)S(1)} %pad_maximum_fusion), channel_id=1, source_target_pairs={{0,1},{1,2},{2,3},{4,5},{5,6},{6,7},{8,9},{9,10},{10,11},{12,13},{... | collective-permute-start | bytes 73736 | tf_op jit(solution)/shard_map/ppermute | solution.py:218
  136.0 0.6 add_convert_fusion.ends_ref
  136.6 4.9 %bands.1 = (bf16[3,2,1152,256]{3,2,1,0:T(8,128)(2,1)}, bf16[3,2,1152,256]{3,2,1,0:T(8,128)(2,1)}) custom-call(bf16[3,3,3,128,128]{4,3,2,1,0:T(8,128)(2,1)} %first_ref.1, bf16[3,3,3,128,128]{4,3,2,1,0:T(8,128)(2,1)} %second_ref.1), custom_call_target="tpu_custom_call" | custom-call | tf_op jit(solution)/shard_map/bands/pallas_call | solution.py:206
  141.5 0.0 collective-permute-done.3.right_ref
  141.5 0.0 copy-start.2
  141.5 0.0 collective-permute-done.2.left_ref
  141.5 0.0 copy-start.3
  141.5 0.0 copy-done
  141.5 0.0 copy-done.1
  141.5 0.6 copy-done.2
  142.1 0.0 copy-done.3
  142.1 10.3 %convolve.1 = bf16[2048,128]{1,0:T(8,128)(2,1)} custom-call(s32[4]{0:T(128)} %add_convert_fusion.ends_ref, bf16[8,64,512]{2,1,0:T(8,128)(2,1)} %bitcast.13, bf16[2,64,512]{2,1,0:T(8,128)(2,1)} %copy-done, bf16[2,64,512]{2,1,0:T(8,128)(2,1)} %copy-done.1, bf16[12,2,512]{2,1,0:T(2,128)(2,1)} %copy-done.3, bf16[12,2,512]{2,1,0:T(2,128)(2,1)} %copy-done.2, ...), custom_call_target="tpu_custom_call" | custom-call | tf_op jit(solution)/shard_map/convolve/pallas_call | solution.py:230
  (4 shorter events, 0.1 us)
Async XLA Ops:
  9.9 103.0 %all-to-all-start = ((bf16[32,528,128]{2,1,0:T(8,128)(2,1)}), bf16[32,528,128]{2,1,0:T(8,128)(2,1)}, u32[]{:S(2)}, u32[]{:S(2)}) async-start(bf16[32,528,128]{2,1,0:T(8,128)(2,1)} %contribute.1), calls=%async_computation | async-start | bytes 8650752 | tf_op jit(solution)/shard_map/all_to_all | solution.py:189
  119.5 5.6 %collective-permute-start = (bf16[2,64,512]{2,1,0:T(8,128)(2,1)S(1)}, bf16[2,64,512]{2,1,0:T(8,128)(2,1)S(1)}, u32[]{:S(2)}, u32[]{:S(2)}) collective-permute-start(bf16[2,64,512]{2,1,0:T(8,128)(2,1)S(1)} %bitcast.17), channel_id=1, source_target_pairs={{0,4},{4,8},{8,12},{12,16},{16,20},{20,24},{24,28},{1,5},{5,9},{9,... | collective-permute-start | bytes 393224 | tf_op jit(solution)/shard_map/ppermute | solution.py:218
  122.9 5.7 %collective-permute-start.1 = (bf16[2,64,512]{2,1,0:T(8,128)(2,1)S(1)}, bf16[2,64,512]{2,1,0:T(8,128)(2,1)S(1)}, u32[]{:S(2)}, u32[]{:S(2)}) collective-permute-start(bf16[2,64,512]{2,1,0:T(8,128)(2,1)S(1)} %bitcast.16), channel_id=1, source_target_pairs={{4,0},{8,4},{12,8},{16,12},{20,16},{24,20},{28,24},{5,1},{9,5},{13... | collective-permute-start | bytes 393224 | tf_op jit(solution)/shard_map/ppermute | solution.py:218
  125.2 16.3 %copy-start = (bf16[2,64,512]{2,1,0:T(8,128)(2,1)}, bf16[2,64,512]{2,1,0:T(8,128)(2,1)S(1)}, u32[]{:S(2)}) copy-start(bf16[2,64,512]{2,1,0:T(8,128)(2,1)S(1)} %collective-permute-done.low_ref) | copy-start | bytes 393220
  128.7 12.9 %copy-start.1 = (bf16[2,64,512]{2,1,0:T(8,128)(2,1)}, bf16[2,64,512]{2,1,0:T(8,128)(2,1)S(1)}, u32[]{:S(2)}) copy-start(bf16[2,64,512]{2,1,0:T(8,128)(2,1)S(1)} %collective-permute-done.1.high_ref) | copy-start | bytes 393220
  128.7 12.8 %collective-permute-start.3 = (bf16[12,2,512]{2,1,0:T(2,128)(2,1)S(1)}, bf16[12,2,512]{2,1,0:T(2,128)(2,1)S(1)}, u32[]{:S(2)}, u32[]{:S(2)}) collective-permute-start(bf16[12,2,512]{2,1,0:T(2,128)(2,1)S(1)} %pad_maximum_fusion.1), channel_id=1, source_target_pairs={{1,0},{2,1},{3,2},{5,4},{6,5},{7,6},{9,8},{10,9},{11,10},{13,12},{... | collective-permute-start | bytes 73736 | tf_op jit(solution)/shard_map/ppermute | solution.py:218
  132.8 8.7 %collective-permute-start.2 = (bf16[12,2,512]{2,1,0:T(2,128)(2,1)S(1)}, bf16[12,2,512]{2,1,0:T(2,128)(2,1)S(1)}, u32[]{:S(2)}, u32[]{:S(2)}) collective-permute-start(bf16[12,2,512]{2,1,0:T(2,128)(2,1)S(1)} %pad_maximum_fusion), channel_id=1, source_target_pairs={{0,1},{1,2},{2,3},{4,5},{5,6},{6,7},{8,9},{9,10},{10,11},{12,13},{... | collective-permute-start | bytes 73736 | tf_op jit(solution)/shard_map/ppermute | solution.py:218
  141.5 0.6 copy-start.2
  141.5 0.6 copy-start.3
where the time goes:
time: 153 us; the launch traced here: 152 us
  waiting for transfers between devices  99.4 us (65%)
  Pallas kernels  27.9 us (18%)
  starting transfers between devices  19 us (12%)
  local copies, waits for them, and re-layouts  5.27 us (3%)
    all_to_all x1, waiting for transfers between devices, shards(): lax.all_to_all(outgoing, ('frames', 'rows'), split_axis=0, concat_axis=0,...  95.9 us
    ppermute x4, starting transfers between devices, shifted(): return lax.ppermute(value, axis, pairs)  11.9 us
    pallas_call x1, Pallas kernels, shards(): pl.pallas_call(convolve_kernel, out_shape=jax.ShapeDtypeStruct((cells * D...  10.3 us
    pallas_call x1, Pallas kernels, shards(): pl.pallas_call(functools.partial(contribute_kernel, devices, capacity, to...  7.16 us
    all_to_all x1, starting transfers between devices, shards(): lax.all_to_all(outgoing, ('frames', 'rows'), split_axis=0, concat_axis=0,...  7.14 us
    pallas_call x1, Pallas kernels, shards(): pl.pallas_call(functools.partial(gather_kernel, devices, capacity, size),...  5.59 us
    pallas_call x1, Pallas kernels, shards(): pl.pallas_call(band_kernel, out_shape=(bands, bands), in_specs=[vmem(), v...  4.9 us
    ppermute x4, waiting for transfers between devices, shifted(): return lax.ppermute(value, axis, pairs)  3.47 us
  transfers between devices with their start and end apart: 5, of which 2 were waited for; matrix products, arithmetic and copies ran while one was open for 1% of the time, Pallas kernels for 3%

commit v1 on v0

v1 whole, which is shorter than its diff:
```python
import functools

import jax
import jax.numpy as jnp
from jax import lax
from jax.experimental import pallas as pl
from jax.experimental.pallas import tpu as pltpu
from jax.sharding import PartitionSpec as P

DEPTH = 4
TX = 8
TY = 64
CORES = 2
PARTS = (1, 1, 1, 1)
LABEL_ROWS = 16
VMEM = pltpu.VMEM
LIMIT = 60 * 1024 * 1024


def vmem():
    return pl.BlockSpec(memory_space=pltpu.VMEM)


def smem():
    return pl.BlockSpec(memory_space=pltpu.SMEM)


def anywhere():
    return pl.BlockSpec(memory_space=pl.ANY)


def params():
    return pltpu.CompilerParams(vmem_limit_bytes=LIMIT)


def arrays(count, rows, channels, dtype=jnp.bfloat16):
    return [jax.ShapeDtypeStruct((rows, channels), dtype)] * count


def split_low(value, count):
    if count & (count - 1) == 0:
        return value >> (count.bit_length() - 1), value & (count - 1)
    return value // count, value % count


def apart(target, source, count):
    if count & (count - 1) == 0:
        return target ^ source
    return (target - source + count) % count


def step_to(source, step, count):
    if count & (count - 1) == 0:
        return source ^ step
    return (source + step) % count


def index_kernel(shape, slots, blocks, *refs):
    n_z, n_y, n_x, n_c = shape
    at_ref = refs[0]
    codes = refs[1 : 1 + n_c]
    index_ref, label_ref, counts, labels = refs[1 + n_c :]
    tiles = n_z * n_y * n_x * n_c
    groups = n_y * n_x
    spare = groups * n_z * slots

    def clear(t, carry):
        counts[t] = 0
        return carry

    lax.fori_loop(0, tiles, clear, 0, unroll=8)

    def blank(s, carry):
        labels[s] = -1
        return carry

    lax.fori_loop(0, spare, blank, 0, unroll=8)
    z, y, x, c = (at_ref[i] for i in range(4))
    pairs = codes[0].shape[0]
    for source in range(n_c):
        ref = codes[source]

        def place(p, carry):
            tile, block = split_low(ref[p], blocks)
            rank = counts[tile]
            counts[tile] = rank + 1
            rest, c_to = split_low(tile, n_c)
            rest, x_to = split_low(rest, n_x)
            z_to, y_to = split_low(rest, n_y)
            group = apart(y_to, y, n_y) * n_x + apart(x_to, x, n_x)
            slot = (group * n_z + apart(z_to, z, n_z)) * slots + rank
            slot = jnp.where(c_to == c, slot, spare)
            index_ref[source * pairs + p] = slot
            labels[slot] = block
            return carry

        lax.fori_loop(0, pairs, place, 0, unroll=4)
    lane = lax.broadcasted_iota(jnp.int32, (LABEL_ROWS, label_ref.shape[1]), 1)
    for g in range(groups):
        row = jnp.full(lane.shape, -1, jnp.int32)
        for k in range(n_z * slots):
            row = jnp.where(lane == k, labels[g * n_z * slots + k], row)
        label_ref[g * LABEL_ROWS : (g + 1) * LABEL_ROWS, :] = row.astype(jnp.float32).astype(jnp.bfloat16)


def contribute_kernel(n_c, groups, per_group, top, spans, first, *refs):
    index_ref = refs[0]
    sources = refs[1 : 1 + n_c]
    features = refs[1 + n_c : 1 + 2 * n_c]
    refs = refs[1 + 2 * n_c :]
    label_ref = refs[0]
    outs = refs[1 : 1 + groups * len(spans)]
    refs = refs[1 + groups * len(spans) :]
    buffers = refs[: len(spans)]
    held, load_sems, store_sems = refs[len(spans) :]
    images = features[0].shape[0]
    begin, rows = spans[0][0], sum(span[1] for span in spans)
    loads = [
        pltpu.make_async_copy(
            sources[s].at[:, pl.ds(begin, rows), :], held.at[pl.ds(s * images * top, images * top)], load_sems.at[s]
        )
        for s in range(n_c)
    ]
    for load in loads:
        load.start()
    for s in range(n_c):
        loads[s].wait()

        def image(b, carry):
            p0 = s * images * top + b * top
            weights = held[pl.ds(p0, top)].reshape(top * rows, held.shape[2])
            product = jnp.dot(weights, features[s][b], preferred_element_type=jnp.float32)
            product = product.astype(jnp.bfloat16)
            for t in range(top):
                slot = index_ref[p0 + t]
                for (start, chunk), buffer in zip(spans, buffers):
                    at = t * rows + start - begin
                    buffer[pl.ds(pl.multiple_of(slot * chunk, chunk), chunk), :] = product[at : at + chunk]
            return carry

        lax.fori_loop(0, images, image, 0, unroll=4)
    copies = []
    for i, ((_, chunk), buffer) in enumerate(zip(spans, buffers)):
        length = per_group * chunk
        for g in range(groups):
            n = i * groups + g
            data = outs[n].at[pl.ds(0, length)] if first else outs[n]
            copies.append(pltpu.make_async_copy(buffer.at[pl.ds(g * length, length)], data, store_sems.at[n]))
            if first:
                copies.append(
                    pltpu.make_async_copy(
                        label_ref.at[pl.ds(g * LABEL_ROWS, LABEL_ROWS)],
                        outs[n].at[pl.ds(length, LABEL_ROWS)],
                        store_sems.at[groups * len(spans) + g],
                    )
                )
    for copy in copies:
        copy.start()
    for copy in copies:
        copy.wait()


def merge_kernel(n_z, groups, slots, chunk, blocks, first, *refs):
    messages = refs[:groups]
    refs = refs[groups:]
    per_group = n_z * slots
    stride = per_group + 1
    if first:
        outs = refs[:n_z]
        plan_ref, total, marks, marks_smem, sem = refs[n_z:]
        for g in range(groups):
            row = messages[g][per_group * chunk :, :].astype(jnp.float32)
            marks[g : g + 1, :] = row[0:1, :].astype(jnp.int32)
        copy = pltpu.make_async_copy(marks, marks_smem, sem)
        copy.start()
    else:
        plan_ref = refs[0]
        outs = refs[2 : 2 + n_z]
        (total,) = refs[2 + n_z :]
    total[...] = jnp.zeros_like(total)
    if first:
        copy.wait()
        for g in range(groups):

            def note(s, count):
                label = marks_smem[g, s]
                plan_ref[g * stride + 1 + count] = s * blocks + jnp.maximum(label, 0)
                return count + (label >= 0).astype(jnp.int32)

            plan_ref[g * stride] = lax.fori_loop(0, per_group, note, 0, unroll=8)
    for g in range(groups):

        def add(n, carry):
            slot, label = split_low(plan_ref[g * stride + 1 + n], blocks)
            step = split_low(slot, slots)[0]
            source = pl.ds(pl.multiple_of(slot * chunk, chunk), chunk)
            target = pl.ds(pl.multiple_of((step * blocks + label) * chunk, chunk), chunk)
            total[target, :] += messages[g][source, :].astype(jnp.float32)
            return carry

        lax.fori_loop(0, plan_ref[g * stride], add, 0)
    rows = blocks * chunk
    for step, out in enumerate(outs):
        out[...] = total[step * rows : (step + 1) * rows, :].astype(jnp.bfloat16)


def finish_kernel(n_z, spans, blocks, size, *refs):
    count = n_z * len(spans)
    parts = refs[:count]
    out_ref, low_ref, high_ref, total = refs[count:]
    for k, (start, chunk) in enumerate(spans):
        for block in range(blocks):
            row = block * chunk
            value = None
            for ref in parts[k * n_z : (k + 1) * n_z]:
                part = ref[row : row + chunk, :].astype(jnp.float32)
                value = part if value is None else value + part
            at = block * size + start
            total[at : at + chunk, :] = value
    cells = total.shape[0] // DEPTH
    channels = total.shape[1]
    for z in range(DEPTH):
        part = total[pl.ds(z, cells, stride=DEPTH), :].astype(jnp.bfloat16)
        lanes = slice(z * channels, (z + 1) * channels)
        out_ref[:, lanes] = part
        low_ref[:, lanes] = part[: 2 * TY]
        high_ref[:, lanes] = part[cells - 2 * TY :]


def band_kernel(first_ref, second_ref, out1_ref, out2_ref):
    channels = first_ref.shape[-1]
    zero = jnp.zeros((channels, channels), jnp.bfloat16)
    for source, target in ((first_ref, out1_ref), (second_ref, out2_ref)):
        for dx in range(3):
            for half in range(2):
                for dy in range(3):
                    for k in range(3):
                        z_in = k + half
                        for j in range(2):
                            dz = z_in - (2 * half + j) + 1
                            value = source[dx, dy, dz] if 0 <= dz < 3 else zero
                            row = (dy * 3 + k) * channels
                            target[dx, half, row : row + channels, j * channels : (j + 1) * channels] = value


def convolve_half(copies, bands, half, out_rows, channels):
    total = None
    for dx in range(3):
        pieces = []
        for dy in range(3):
            piece = copies[dy][dx : dx + out_rows, :, half * channels : (half + 3) * channels]
            pieces.append(piece.reshape(-1, 3 * channels))
        product = jnp.dot(
            jnp.concatenate(pieces, axis=1), bands[dx, half], preferred_element_type=jnp.float32
        )
        total = product if total is None else total + product
    return total


def silu(v):
    return v / (1.0 + jnp.exp(-v))


def convolve_kernel(
    ends_ref, main_ref, low_ref, high_ref, left_ref, right_ref,
    band1_ref, band2_ref, bias1_ref, bias2_ref, out_ref,
    copies0, copies1, copies2, hidden, shift1, shift2, stage,
):
    channels = bias1_ref.shape[1]
    rows, cols = main_ref.shape[0], main_ref.shape[1]
    for x0, source in ((0, low_ref), (2, main_ref), (2 + rows, high_ref)):
        value = source[...]
        part = slice(x0, x0 + value.shape[0])
        copies0[part, 2 : 2 + cols, :] = value
        copies1[part, 1 : 1 + cols, :] = value
        copies2[part, 0:cols, :] = value
    left = left_ref[...]
    right = right_ref[...]
    copies0[:, 0:2, :] = left
    copies1[:, 0:1, :] = left[:, 1:2]
    copies1[:, 1 + cols : 2 + cols, :] = right[:, 0:1]
    copies2[:, cols : 2 + cols, :] = right
    for half in range(2):
        total = convolve_half((copies0, copies1, copies2), band1_ref, half, rows + 2, channels)
        bias = jnp.concatenate([bias1_ref[...], bias1_ref[...]], axis=1)
        value = silu(total + bias).reshape(rows + 2, -1, 2 * channels)
        x_at = lax.broadcasted_iota(jnp.int32, value.shape, 0)
        y_at = lax.broadcasted_iota(jnp.int32, value.shape, 1)
        keep = (x_at >= ends_ref[0]) & (x_at < rows + 2 - ends_ref[1])
        keep = keep & (y_at >= ends_ref[2]) & (y_at < cols + 2 - ends_ref[3])
        value = jnp.where(keep, value, 0.0).astype(jnp.bfloat16)
        hidden[:, :, half * 2 * channels : (half + 1) * 2 * channels] = value
    shift1[...] = hidden[:, 1 : 1 + cols, :]
    shift2[...] = hidden[:, 2 : 2 + cols, :]
    for half in range(2):
        total = convolve_half(
            (hidden.at[:, 0:cols, :], shift1, shift2), band2_ref, half, rows, channels
        )
        for j in range(2):
            value = silu(total[:, j * channels : (j + 1) * channels] + bias2_ref[...])
            stage[pl.ds(2 * half + j, rows * cols, stride=DEPTH), :] = value
    out_ref[...] = stage[...].astype(jnp.bfloat16)


def shards(features, pair_weight, target_tile, target_block, conv1_weight, conv1_bias, conv2_weight, conv2_bias):
    images, size, channels = features.shape[1:]
    top = target_tile.shape[2]
    n_frames = lax.axis_size("frames")
    n_rows = lax.axis_size("rows")
    devices = n_frames * n_rows
    capacity = max(2, 2 * images * top // devices)
    blocks = TX * TY * DEPTH // size
    n_c = CORES if n_rows % CORES == 0 else 1
    n_x = n_rows // n_c
    n_y = n_x if n_frames % n_x == 0 else 1
    n_z = n_frames // n_y
    shape = (n_z, n_y, n_x, n_c)
    groups = n_y * n_x
    slots = n_c * capacity
    per_group = n_z * slots
    stride = per_group + 1
    spans, start = [], 0
    for part in PARTS:
        spans.append((start * size // sum(PARTS), part * size // sum(PARTS)))
        start += part

    def moved_by(value, dz=0, dy=0, dx=0, dc=0):
        pairs = []
        for source in range(devices):
            f, r = divmod(source, n_rows)
            z, y = divmod(f, n_y)
            x, c = divmod(r, n_c)
            z, y, x = step_to(z, dz, n_z), step_to(y, dy, n_y), step_to(x, dx, n_x)
            c = step_to(c, dc, n_c)
            pairs.append((source, ((z * n_y + y) * n_x + x) * n_c + c))
        return lax.ppermute(value, ("frames", "rows"), pairs)

    f, r = lax.axis_index("frames"), lax.axis_index("rows")
    at = jnp.stack([f // n_y, f % n_y, r // n_c, r % n_c]).astype(jnp.int32)
    code = (target_tile * blocks + target_block).reshape(-1)
    weights = pair_weight[0].reshape(images * top, size, size)
    shared = [(weights, features[0], code)]
    for dc in range(1, n_c):
        shared.append(tuple(moved_by(v, dc=dc) for v in (weights, features[0], code)))
    index, labels = pl.pallas_call(
        functools.partial(index_kernel, shape, slots, blocks),
        out_shape=(
            jax.ShapeDtypeStruct((n_c * images * top,), jnp.int32),
            jax.ShapeDtypeStruct((groups * LABEL_ROWS, channels), jnp.bfloat16),
        ),
        in_specs=[smem()] * (1 + n_c),
        out_specs=(smem(), vmem()),
        scratch_shapes=[pltpu.SMEM((devices,), jnp.int32), pltpu.SMEM((groups * per_group + 1,), jnp.int32)],
        compiler_params=params(),
        name="index",
    )(at, *[v[2] for v in shared])

    def contribute(ks):
        own = [spans[k] for k in ks]
        first = ks[0] == 0
        outs, scratch = [], []
        for _, chunk in own:
            outs += arrays(groups, per_group * chunk + (LABEL_ROWS if first else 0), channels)
            scratch.append(VMEM(((groups * per_group + 1) * chunk, channels), jnp.bfloat16))
        rows = sum(chunk for _, chunk in own)
        scratch += [
            VMEM((n_c * images * top, rows, size), jnp.bfloat16),
            pltpu.SemaphoreType.DMA((n_c,)),
            pltpu.SemaphoreType.DMA((len(outs) + groups,)),
        ]
        made = pl.pallas_call(
            functools.partial(contribute_kernel, n_c, groups, per_group, top, own, first),
            out_shape=tuple(outs),
            in_specs=[smem()] + [anywhere()] * n_c + [vmem()] * (n_c + 1),
            out_specs=(anywhere(),) * len(outs),
            scratch_shapes=scratch,
            compiler_params=params(),
        )(index, *[v[0] for v in shared], *[v[1] for v in shared], labels)
        for i, k in enumerate(ks):
            messages[k] = made[i * groups : (i + 1) * groups]

    def exchange(k):
        return [
            moved_by(value, dy=g // n_x, dx=g % n_x) if g else value
            for g, value in enumerate(messages[k])
        ]

    def merge(k, received, plan, after):
        first = k == 0
        chunk = spans[k][1]
        outs = arrays(n_z, blocks * chunk, channels)
        out_specs = [vmem()] * n_z
        scratch = [VMEM((n_z * blocks * chunk, channels), jnp.float32)]
        in_specs = [vmem()] * groups
        args = tuple(received)
        if first:
            outs.append(jax.ShapeDtypeStruct((stride * groups,), jnp.int32))
            out_specs.append(smem())
            scratch += [
                VMEM((groups, channels), jnp.int32),
                pltpu.SMEM((groups, channels), jnp.int32),
                pltpu.SemaphoreType.DMA,
            ]
        else:
            in_specs += [smem(), anywhere()]
            args += (plan, after)
        return pl.pallas_call(
            functools.partial(merge_kernel, n_z, groups, slots, chunk, blocks, first),
            out_shape=tuple(outs),
            in_specs=in_specs,
            out_specs=tuple(out_specs),
            scratch_shapes=scratch,
            compiler_params=params(),
        )(*args)

    bands = jax.ShapeDtypeStruct((3, 2, 9 * channels, 2 * channels), jnp.bfloat16)
    band1, band2 = pl.pallas_call(
        band_kernel,
        out_shape=(bands, bands),
        in_specs=[vmem(), vmem()],
        out_specs=(vmem(), vmem()),
        compiler_params=params(),
        name="bands",
    )(conv1_weight, conv2_weight)
    messages = {}
    contribute([0])
    contribute(list(range(1, len(spans))))
    plan, final = None, []
    for k in range(len(spans)):
        merged = merge(k, exchange(k), plan, band1)
        if k == 0:
            plan = merged[-1]
        final += [moved_by(part, dz=dz) if dz else part for dz, part in enumerate(merged[:n_z])]
    cells = TX * TY
    lanes = DEPTH * channels
    main, first_rows, last_rows = pl.pallas_call(
        functools.partial(finish_kernel, n_z, spans, blocks, size),
        out_shape=(
            jax.ShapeDtypeStruct((cells, lanes), jnp.bfloat16),
            jax.ShapeDtypeStruct((2 * TY, lanes), jnp.bfloat16),
            jax.ShapeDtypeStruct((2 * TY, lanes), jnp.bfloat16),
        ),
        in_specs=[vmem()] * len(final),
        out_specs=(vmem(),) * 3,
        scratch_shapes=[VMEM((cells * DEPTH, channels), jnp.float32)],
        compiler_params=params(),
        name="finish",
    )(*final)
    main = main.reshape(TX, TY, lanes)

    def moved(value, axis, count, step):
        pairs = [(i, i + step) for i in range(count) if 0 <= i + step < count]
        return lax.ppermute(value, axis, pairs)

    low = moved(last_rows.reshape(2, TY, lanes), "frames", n_frames, 1)
    high = moved(first_rows.reshape(2, TY, lanes), "frames", n_frames, -1)
    edge = jnp.concatenate([low[:, TY - 2 :], main[:, TY - 2 :], high[:, TY - 2 :]], axis=0)
    left = moved(edge, "rows", n_rows, 1)
    edge = jnp.concatenate([low[:, :2], main[:, :2], high[:, :2]], axis=0)
    right = moved(edge, "rows", n_rows, -1)
    ends = jnp.stack([f == 0, f == n_frames - 1, r == 0, r == n_rows - 1]).astype(jnp.int32)
    wide = 80
    out = pl.pallas_call(
        convolve_kernel,
        out_shape=jax.ShapeDtypeStruct((cells * DEPTH, channels), jnp.bfloat16),
        in_specs=[smem()] + [vmem()] * 9,
        out_specs=vmem(),
        scratch_shapes=[VMEM((TX + 4, wide, lanes), jnp.bfloat16)] * 3
        + [VMEM((TX + 2, wide, lanes), jnp.bfloat16)]
        + [VMEM((TX + 2, TY, lanes), jnp.bfloat16)] * 2
        + [VMEM((cells * DEPTH, channels), jnp.float32)],
        compiler_params=params(),
        name="convolve",
    )(ends, main, low, high, left, right, band1, band2, conv1_bias[None], conv2_bias[None])
    return out.reshape(TX, TY, DEPTH, channels)


def solution(mesh):
    placed = (
        P("frames", "rows", None, None),
        P("frames", "rows", None, None, None),
        P("frames", "rows", None),
        P("frames", "rows", None),
        P(),
        P(),
        P(),
        P(),
    )
    return jax.shard_map(
        shards,
        mesh=mesh,
        in_specs=placed,
        out_specs=P("frames", "rows", None, None),
        check_vma=False,
    )
```

time: 153 us -> 143 us (0.935)
  waiting for transfers between devices: 99.4 us -> 43.6 us
  starting transfers between devices: 19 us -> 47.4 us
  Pallas kernels: 27.9 us -> 44.3 us
    all_to_all x1 -> x0, waiting for transfers between devices: 95.9 us -> none  [shards(): lax.all_to_all(outgoing, ('frames', 'rows'), split_axis=0, concat_axis=0,...]
    ppermute x4 -> x31, waiting for transfers between devices: 3.47 us -> 43.6 us  [the longest x27 33.9 us: moved_by(): return lax.ppermute(value, ('frames', 'rows'), pairs)]
    ppermute x4 -> x31, starting transfers between devices: 11.9 us -> 47.4 us  [the longest x27 37.2 us: moved_by(): return lax.ppermute(value, ('frames', 'rows'), pairs)]
    pallas_call x2 -> x8, Pallas kernels: 12.7 us -> 29.3 us  [the longest x4 12.6 us: merge(): pl.pallas_call(functools.partial(merge_kernel, n_z, groups, slots, chunk,...]
    all_to_all x1 -> x0, starting transfers between devices: 7.14 us -> none  [shards(): lax.all_to_all(outgoing, ('frames', 'rows'), split_axis=0, concat_axis=0,...]
    unnamed x10 -> x82, local copies, waits for them, and re-layouts: 2.12 us -> 3.31 us
  transfers between devices with their start and end apart: 5 -> 31, of which waited for: 2 -> 10; matrix products, arithmetic and copies ran while one was open for 1% -> 2% of each run, Pallas kernels for 3% -> 17%
where the time goes in v1:
time: 143 us; the launch traced here: 142 us
  starting transfers between devices  47.4 us (33%)
  Pallas kernels  44.3 us (31%)
  waiting for transfers between devices  43.6 us (30%)
  local copies, waits for them, and re-layouts  4.41 us (3%)
  other arithmetic  2.05 us (1%)
    ppermute x27, starting transfers between devices, moved_by(): return lax.ppermute(value, ('frames', 'rows'), pairs)  37.2 us
    ppermute x27, waiting for transfers between devices, moved_by(): return lax.ppermute(value, ('frames', 'rows'), pairs)  33.9 us
    pallas_call x4, Pallas kernels, merge(): pl.pallas_call(functools.partial(merge_kernel, n_z, groups, slots, chunk,...  12.6 us
    pallas_call x2, Pallas kernels, contribute(): pl.pallas_call(functools.partial(contribute_kernel, n_c, groups, per_grou...  11.3 us
    pallas_call x1, Pallas kernels, shards(): pl.pallas_call(convolve_kernel, out_shape=jax.ShapeDtypeStruct((cells * D...  10.2 us
    ppermute x4, starting transfers between devices, moved(): return lax.ppermute(value, axis, pairs)  10.2 us
    ppermute x4, waiting for transfers between devices, moved(): return lax.ppermute(value, axis, pairs)  9.68 us
    pallas_call x1, Pallas kernels, shards(): pl.pallas_call(band_kernel, out_shape=(bands, bands), in_specs=[vmem(), v...  4.83 us
  transfers between devices with their start and end apart: 31, of which 10 were waited for; matrix products, arithmetic and copies ran while one was open for 2% of the time, Pallas kernels for 17%

profile of v1, /device:TPU:1, one launch (start us, length us, event | category | flops | bytes accessed | tf_op | source)
XLA Modules:
  0.0 142.2 jit_solution(14375123238971975175)
XLA Ops:
  0.0 0.0 collective-permute-start.1
  0.0 0.5 collective-permute-start.2
  0.5 0.7 multiply_add_fusion
  1.2 0.1 copy.10
  1.3 0.1 reshape.15.refs_1_
  1.4 0.1 collective-permute-start
  1.5 0.7 pad_add_fusion.refs_0_
  2.2 3.0 %collective-permute-done.refs_2_ = s32[64]{0:T(128)S(1)} collective-permute-done((s32[64]{0:T(128)S(1)}, s32[64]{0:T(128)S(1)}, u32[]{:S(2)}, u32[]{:S(2)}) %collective-permute-start) | collective-permute-done | bytes 288 | tf_op jit(solution)/shard_map/ppermute | solution.py:336
  5.1 0.5 copy-done.40
  5.6 2.6 %index.1 = (s32[128]{0:T(128)}, bf16[64,128]{1,0:T(8,128)(2,1)}) custom-call(s32[4]{0:T(128)} %pad_add_fusion.refs_0_, s32[64]{0:T(128)} %copy-done.30, s32[64]{0:T(128)} %copy-done.40), custom_call_target="tpu_custom_call" | custom-call | tf_op jit(solution)/shard_map/index/pallas_call | solution.py:345
  8.3 0.0 copy-start.1
  8.3 0.8 copy-done.1
  9.1 0.7 copy-done
  9.7 6.5 %shard_map.84 = (bf16[1024,128]{1,0:T(8,128)(2,1)}, bf16[1024,128]{1,0:T(8,128)(2,1)}, bf16[1024,128]{1,0:T(8,128)(2,1)}, bf16[1024,128]{1,0:T(8,128)(2,1)}, bf1...) custom-call(s32[128]{0:T(128)} %get-tuple-element.45.refs_0_, ...), custom_call_target="tpu_custom_call" | custom-call | tf_op jit(solution)/shard_map/pallas_call | solution.py:371
  16.3 2.4 %collective-permute-start.15 = (bf16[1024,128]{1,0:T(8,128)(2,1)}, bf16[1024,128]{1,0:T(8,128)(2,1)S(1)}, u32[]{:S(2)}, u32[]{:S(2)}) collective-permute-start(bf16[1024,128]{1,0:T(8,128)(2,1)} %get-tuple-element.66), channel_id=1, source_target_pairs={{0,2},{1,3},{2,0},{3,1},{4,6},{5,7},{6,4},{7,5},{8,10},{9,11},{10,... | collective-permute-start | bytes 786440 | tf_op jit(solution)/shard_map/ppermute | solution.py:336
  18.7 1.2 collective-permute-start.16
  19.9 0.0 collective-permute-start.17
  20.0 1.4 collective-permute-start.21
  21.4 4.8 %shard_map.82 = (bf16[1040,128]{1,0:T(8,128)(2,1)}, bf16[1040,128]{1,0:T(8,128)(2,1)}, bf16[1040,128]{1,0:T(8,128)(2,1)}, bf16[1040,128]{1,0:T(8,128)(2,1)}) custom-call(s32[128]{0:T(128)} %get-tuple-element.45.refs_0_, bf16[64,128,128]{2,1,0:T(8,128)(2,1)} %bitcast.18, bf16[64,128,128]{2,1,0:T(8,128)(2,1)} %copy-done, bf16[16,128,128]{2,1,0:T(8,128)(2,1)} %bitcast.21, ...), custom_call_target="tpu_custom_call" | custom-call | tf_op jit(solution)/shard_map/pallas_call | solution.py:371
  26.2 0.1 collective-permute-start.3
  26.3 1.4 collective-permute-start.4
  27.7 1.2 collective-permute-start.5
  28.9 2.9 %collective-permute-done.17.refs_3_ = bf16[1024,128]{1,0:T(8,128)(2,1)S(1)} collective-permute-done((bf16[1024,128]{1,0:T(8,128)(2,1)}, bf16[1024,128]{1,0:T(8,128)(2,1)S(1)}, u32[]{:S(2)}, u32[]{:S(2)}) %collective-permute-start.17) | collective-permute-done | bytes 262176 | tf_op jit(solution)/shard_map/ppermute | solution.py:336
  31.8 1.1 collective-permute-start.22
  32.9 3.6 %collective-permute-done.21.refs_1_ = bf16[1024,128]{1,0:T(8,128)(2,1)S(1)} collective-permute-done((bf16[1024,128]{1,0:T(8,128)(2,1)}, bf16[1024,128]{1,0:T(8,128)(2,1)S(1)}, u32[]{:S(2)}, u32[]{:S(2)}) %collective-permute-start.21) | collective-permute-done | bytes 262176 | tf_op jit(solution)/shard_map/ppermute | solution.py:336
  36.5 2.1 %collective-permute-start.23 = (bf16[1024,128]{1,0:T(8,128)(2,1)}, bf16[1024,128]{1,0:T(8,128)(2,1)S(1)}, u32[]{:S(2)}, u32[]{:S(2)}) collective-permute-start(bf16[1024,128]{1,0:T(8,128)(2,1)} %get-tuple-element.76), channel_id=1, source_target_pairs={{0,6},{1,7},{2,4},{3,5},{4,2},{5,3},{6,0},{7,1},{8,14},{9,15},{10,... | collective-permute-start | bytes 786440 | tf_op jit(solution)/shard_map/ppermute | solution.py:336
  38.6 3.6 %collective-permute-done.3.refs_1_ = bf16[1040,128]{1,0:T(8,128)(2,1)S(1)} collective-permute-done((bf16[1040,128]{1,0:T(8,128)(2,1)}, bf16[1040,128]{1,0:T(8,128)(2,1)S(1)}, u32[]{:S(2)}, u32[]{:S(2)}) %collective-permute-start.3) | collective-permute-done | bytes 266272 | tf_op jit(solution)/shard_map/ppermute | solution.py:336
  42.2 1.2 collective-permute-start.9
  43.4 1.3 collective-permute-start.10
  44.7 4.2 %collective-permute-done.5.refs_3_ = bf16[1040,128]{1,0:T(8,128)(2,1)S(1)} collective-permute-done((bf16[1040,128]{1,0:T(8,128)(2,1)}, bf16[1040,128]{1,0:T(8,128)(2,1)S(1)}, u32[]{:S(2)}, u32[]{:S(2)}) %collective-permute-start.5) | collective-permute-done | bytes 266272 | tf_op jit(solution)/shard_map/ppermute | solution.py:336
  48.9 1.2 collective-permute-start.11
  50.1 4.0 %shard_map.83 = (bf16[512,128]{1,0:T(8,128)(2,1)}, bf16[512,128]{1,0:T(8,128)(2,1)}, bf16[512,128]{1,0:T(8,128)(2,1)}, bf16[512,128]{1,0:T(8,128)(2,1)}, s32[132]{0:T(256)}) custom-call(bf16[1040,128]{1,0:T(8,128)(2,1)} %get-tuple-element.47.refs_0_, bf16[1040,128]{1,0:T(8,128)(2,1)} %copy-done.2, bf16[1040,128]{1,0:T(8,128)(2,1)} %copy-done.3, ...), custom_call_target="tpu_custom_call" | custom-call | tf_op jit(solution)/shard_map/pallas_call | solution.py:407
  54.1 1.4 collective-permute-start.6
  55.5 2.3 %collective-permute-start.7 = (bf16[512,128]{1,0:T(8,128)(2,1)}, bf16[512,128]{1,0:T(8,128)(2,1)S(1)}, u32[]{:S(2)}, u32[]{:S(2)}) collective-permute-start(bf16[512,128]{1,0:T(8,128)(2,1)} %get-tuple-element.53), channel_id=1, source_target_pairs={{0,16},{1,17},{2,18},{3,19},{4,20},{5,21},{6,22},{7,23},{8,24},{9,... | collective-permute-start | bytes 393224 | tf_op jit(solution)/shard_map/ppermute | solution.py:336
  57.8 4.8 %bands.1 = (bf16[3,2,1152,256]{3,2,1,0:T(8,128)(2,1)}, bf16[3,2,1152,256]{3,2,1,0:T(8,128)(2,1)}) custom-call(bf16[3,3,3,128,128]{4,3,2,1,0:T(8,128)(2,1)} %first_ref.1, bf16[3,3,3,128,128]{4,3,2,1,0:T(8,128)(2,1)} %second_ref.1), custom_call_target="tpu_custom_call" | custom-call | tf_op jit(solution)/shard_map/bands/pallas_call | solution.py:417
  62.6 2.9 %shard_map.87 = (bf16[512,128]{1,0:T(8,128)(2,1)}, bf16[512,128]{1,0:T(8,128)(2,1)}, bf16[512,128]{1,0:T(8,128)(2,1)}, bf16[512,128]{1,0:T(8,128)(2,1)}) custom-call(bf16[1024,128]{1,0:T(8,128)(2,1)} %get-tuple-element.73.refs_0_, bf16[1024,128]{1,0:T(8,128)(2,1)} %copy-done.9, bf16[1024,128]{1,0:T(8,128)(2,1)} %copy-done.12, bf16[1024,128]{1,0:T(8,128)(2,1)} %copy-done.13, ...), custom_call_target="tpu_custom_call" | custom-call | tf_op jit(solution)/shard_map/pallas_call | solution.py:407
  65.5 2.9 %shard_map.86 = (bf16[512,128]{1,0:T(8,128)(2,1)}, bf16[512,128]{1,0:T(8,128)(2,1)}, bf16[512,128]{1,0:T(8,128)(2,1)}, bf16[512,128]{1,0:T(8,128)(2,1)}) custom-call(bf16[1024,128]{1,0:T(8,128)(2,1)} %get-tuple-element.65.refs_0_, bf16[1024,128]{1,0:T(8,128)(2,1)} %copy-done.5, bf16[1024,128]{1,0:T(8,128)(2,1)} %copy-done.6, bf16[1024,128]{1,0:T(8,128)(2,1)} %copy-done.7, ...), custom_call_target="tpu_custom_call" | custom-call | tf_op jit(solution)/shard_map/pallas_call | solution.py:407
  68.5 0.2 collective-permute-start.8
  68.7 0.3 collective-permute-start.24
  69.0 3.2 %collective-permute-start.25 = (bf16[512,128]{1,0:T(8,128)(2,1)S(1)}, bf16[512,128]{1,0:T(8,128)(2,1)S(1)}, u32[]{:S(2)}, u32[]{:S(2)}) collective-permute-start(bf16[512,128]{1,0:T(8,128)(2,1)S(1)} %copy-done.38), channel_id=1, source_target_pairs={{0,16},{1,17},{2,18},{3,19},{4,20},{5,21},{6,22},{7,23},{8,24},{9,... | collective-permute-start | bytes 393224 | tf_op jit(solution)/shard_map/ppermute | solution.py:336
  72.2 0.2 collective-permute-start.26
  72.4 0.2 collective-permute-start.18
  72.6 2.8 %shard_map.85 = (bf16[512,128]{1,0:T(8,128)(2,1)}, bf16[512,128]{1,0:T(8,128)(2,1)}, bf16[512,128]{1,0:T(8,128)(2,1)}, bf16[512,128]{1,0:T(8,128)(2,1)}) custom-call(bf16[1024,128]{1,0:T(8,128)(2,1)} %get-tuple-element.55.refs_0_, bf16[1024,128]{1,0:T(8,128)(2,1)} %copy-done.8, bf16[1024,128]{1,0:T(8,128)(2,1)} %copy-done.10, bf16[1024,128]{1,0:T(8,128)(2,1)} %copy-done.11, ...), custom_call_target="tpu_custom_call" | custom-call | tf_op jit(solution)/shard_map/pallas_call | solution.py:407
  75.4 3.3 %collective-permute-start.19 = (bf16[512,128]{1,0:T(8,128)(2,1)S(1)}, bf16[512,128]{1,0:T(8,128)(2,1)S(1)}, u32[]{:S(2)}, u32[]{:S(2)}) collective-permute-start(bf16[512,128]{1,0:T(8,128)(2,1)S(1)} %copy-done.35), channel_id=1, source_target_pairs={{0,16},{1,17},{2,18},{3,19},{4,20},{5,21},{6,22},{7,23},{8,24},{9,... | collective-permute-start | bytes 393224 | tf_op jit(solution)/shard_map/ppermute | solution.py:336
  78.7 0.2 collective-permute-start.20
  78.9 2.1 %collective-permute-done.25.refs_14_ = bf16[512,128]{1,0:T(8,128)(2,1)S(1)} collective-permute-done((bf16[512,128]{1,0:T(8,128)(2,1)S(1)}, bf16[512,128]{1,0:T(8,128)(2,1)S(1)}, u32[]{:S(2)}, u32[]{:S(2)}) %collective-permute-start.25) | collective-permute-done | bytes 131104 | tf_op jit(solution)/shard_map/ppermute | solution.py:336
  81.1 10.4 %collective-permute-start.13 = (bf16[512,128]{1,0:T(8,128)(2,1)}, bf16[512,128]{1,0:T(8,128)(2,1)S(1)}, u32[]{:S(2)}, u32[]{:S(2)}) collective-permute-start(bf16[512,128]{1,0:T(8,128)(2,1)} %get-tuple-element.63), channel_id=1, source_target_pairs={{0,16},{1,17},{2,18},{3,19},{4,20},{5,21},{6,22},{7,23},{8,24},{9,... | collective-permute-start | bytes 393224 | tf_op jit(solution)/shard_map/ppermute | solution.py:336
  91.5 0.3 collective-permute-start.14
  91.9 5.2 %collective-permute-done.19.refs_10_ = bf16[512,128]{1,0:T(8,128)(2,1)S(1)} collective-permute-done((bf16[512,128]{1,0:T(8,128)(2,1)S(1)}, bf16[512,128]{1,0:T(8,128)(2,1)S(1)}, u32[]{:S(2)}, u32[]{:S(2)}) %collective-permute-start.19) | collective-permute-done | bytes 131104 | tf_op jit(solution)/shard_map/ppermute | solution.py:336
  97.1 9.2 %collective-permute-done.13.refs_6_ = bf16[512,128]{1,0:T(8,128)(2,1)S(1)} collective-permute-done((bf16[512,128]{1,0:T(8,128)(2,1)}, bf16[512,128]{1,0:T(8,128)(2,1)S(1)}, u32[]{:S(2)}, u32[]{:S(2)}) %collective-permute-start.13) | collective-permute-done | bytes 131104 | tf_op jit(solution)/shard_map/ppermute | solution.py:336
  106.5 0.6 copy-done.26
  107.0 0.1 copy-done.27
  107.1 2.8 %finish.1 = (bf16[512,512]{1,0:T(8,128)(2,1)}, bf16[128,512]{1,0:T(8,128)(2,1)}, bf16[128,512]{1,0:T(8,128)(2,1)}) custom-call(bf16[512,128]{1,0:T(8,128)(2,1)} %get-tuple-element.51.refs_0_, bf16[512,128]{1,0:T(8,128)(2,1)} %copy-done.16, bf16[512,128]{1,0:T(8,128)(2,1)} %copy-done.17, bf16[512,128]{1,0:T(8,128)(2,1)} %copy-done.18, ...), custom_call_target="tpu_custom_call" | custom-call | tf_op jit(solution)/shard_map/finish/pallas_call | solution.py:436
  109.8 1.3 collective-permute-start.27
  111.1 1.3 collective-permute-start.28
  112.4 0.9 fusion
  113.3 0.0 collective-permute-done.27.low_ref
  113.4 7.0 %collective-permute-done.28.high_ref = bf16[2,64,512]{2,1,0:T(8,128)(2,1)S(1)} collective-permute-done((bf16[2,64,512]{2,1,0:T(8,128)(2,1)}, bf16[2,64,512]{2,1,0:T(8,128)(2,1)S(1)}, u32[]{:S(2)}, u32[]{:S(2)}) %collective-permute-start.28) | collective-permute-done | bytes 131104 | tf_op jit(solution)/shard_map/ppermute | solution.py:453
  120.5 5.7 %collective-permute-start.29 = (bf16[12,2,512]{2,1,0:T(2,128)(2,1)S(1)}, bf16[12,2,512]{2,1,0:T(2,128)(2,1)S(1)}, u32[]{:S(2)}, u32[]{:S(2)}) collective-permute-start(bf16[12,2,512]{2,1,0:T(2,128)(2,1)S(1)} %pad_maximum_fusion), channel_id=1, source_target_pairs={{0,1},{1,2},{2,3},{4,5},{5,6},{6,7},{8,9},{9,10},{10,11},{12,13},{... | collective-permute-start | bytes 73736 | tf_op jit(solution)/shard_map/ppermute | solution.py:453
  126.2 1.9 %collective-permute-start.30 = (bf16[12,2,512]{2,1,0:T(2,128)(2,1)S(1)}, bf16[12,2,512]{2,1,0:T(2,128)(2,1)S(1)}, u32[]{:S(2)}, u32[]{:S(2)}) collective-permute-start(bf16[12,2,512]{2,1,0:T(2,128)(2,1)S(1)} %pad_maximum_fusion.1), channel_id=1, source_target_pairs={{1,0},{2,1},{3,2},{5,4},{6,5},{7,6},{9,8},{10,9},{11,10},{13,12},{... | collective-permute-start | bytes 73736 | tf_op jit(solution)/shard_map/ppermute | solution.py:453
  128.2 0.6 add_convert_fusion.ends_ref
  128.8 2.6 %collective-permute-done.30.right_ref = bf16[12,2,512]{2,1,0:T(2,128)(2,1)S(1)} collective-permute-done((bf16[12,2,512]{2,1,0:T(2,128)(2,1)S(1)}, bf16[12,2,512]{2,1,0:T(2,128)(2,1)S(1)}, u32[]{:S(2)}, u32[]{:S(2)}) %collective-permute-start.30) | collective-permute-done | bytes 24608 | tf_op jit(solution)/shard_map/ppermute | solution.py:453
  131.4 0.6 copy-done.29
  132.0 10.2 %convolve.1 = bf16[2048,128]{1,0:T(8,128)(2,1)} custom-call(s32[4]{0:T(128)} %add_convert_fusion.ends_ref, bf16[8,64,512]{2,1,0:T(8,128)(2,1)} %bitcast.23, bf16[2,64,512]{2,1,0:T(8,128)(2,1)} %copy-done.14, bf16[2,64,512]{2,1,0:T(8,128)(2,1)} %copy-done.15, bf16[12,2,512]{2,1,0:T(2,128)(2,1)} %copy-done.28, bf16[12,2,512]{2,1,0:T(2,128)(2,1)} %copy-done.29, ...), custom_call_target="tpu_custom_call" | custom-call | tf_op jit(solution)/shard_map/convolve/pallas_call | solution.py:463
  (100 shorter events, 0.3 us)
Async XLA Ops:
  0.0 8.3 %collective-permute-start.1 = (bf16[64,128,128]{2,1,0:T(8,128)(2,1)}, bf16[64,128,128]{2,1,0:T(8,128)(2,1)S(1)}, u32[]{:S(2)}, u32[]{:S(2)}) collective-permute-start(bf16[64,128,128]{2,1,0:T(8,128)(2,1)} %bitcast.16), channel_id=1, source_target_pairs={{0,1},{1,0},{2,3},{3,2},{4,5},{5,4},{6,7},{7,6},{8,9},{9,8},{10,11... | collective-permute-start | bytes 6291464 | tf_op jit(solution)/shard_map/ppermute | solution.py:336
  0.0 8.2 %collective-permute-start.2 = (bf16[16,128,128]{2,1,0:T(8,128)(2,1)}, bf16[16,128,128]{2,1,0:T(8,128)(2,1)S(1)}, u32[]{:S(2)}, u32[]{:S(2)}) collective-permute-start(bf16[16,128,128]{2,1,0:T(8,128)(2,1)} %bitcast.19), channel_id=1, source_target_pairs={{0,1},{1,0},{2,3},{3,2},{4,5},{5,4},{6,7},{7,6},{8,9},{9,8},{10,11... | collective-permute-start | bytes 1572872 | tf_op jit(solution)/shard_map/ppermute | solution.py:336
  1.4 3.7 %copy-start.30 = (s32[64]{0:T(128)}, s32[64]{0:T(128)S(1)}, u32[]{:S(2)}) copy-start(s32[64]{0:T(128)S(1)} %reshape.15.refs_1_) | copy-start | bytes 772
  1.4 3.7 %collective-permute-start = (s32[64]{0:T(128)S(1)}, s32[64]{0:T(128)S(1)}, u32[]{:S(2)}, u32[]{:S(2)}) collective-permute-start(s32[64]{0:T(128)S(1)} %reshape.15.refs_1_), channel_id=1, source_target_pairs={{0,1},{1,0},{2,3},{3,2},{4,5},{5,4},{6,7},{7,6},{8,9},{9,8},{10,11... | collective-permute-start | bytes 776 | tf_op jit(solution)/shard_map/ppermute | solution.py:336
  16.3 25.9 %copy-start.33 = (bf16[1024,128]{1,0:T(8,128)(2,1)S(1)}, bf16[1024,128]{1,0:T(8,128)(2,1)}, u32[]{:S(2)}) copy-start(bf16[1024,128]{1,0:T(8,128)(2,1)} %get-tuple-element.56) | copy-start | bytes 786436
  16.3 27.1 %copy-start.32 = (bf16[1024,128]{1,0:T(8,128)(2,1)S(1)}, bf16[1024,128]{1,0:T(8,128)(2,1)}, u32[]{:S(2)}) copy-start(bf16[1024,128]{1,0:T(8,128)(2,1)} %get-tuple-element.57) | copy-start | bytes 786436
  16.3 32.6 %copy-start.31 = (bf16[1024,128]{1,0:T(8,128)(2,1)S(1)}, bf16[1024,128]{1,0:T(8,128)(2,1)}, u32[]{:S(2)}) copy-start(bf16[1024,128]{1,0:T(8,128)(2,1)} %get-tuple-element.58) | copy-start | bytes 786436
  16.3 10.0 %collective-permute-start.15 = (bf16[1024,128]{1,0:T(8,128)(2,1)}, bf16[1024,128]{1,0:T(8,128)(2,1)S(1)}, u32[]{:S(2)}, u32[]{:S(2)}) collective-permute-start(bf16[1024,128]{1,0:T(8,128)(2,1)} %get-tuple-element.66), channel_id=1, source_target_pairs={{0,2},{1,3},{2,0},{3,1},{4,6},{5,7},{6,4},{7,5},{8,10},{9,11},{10,... | collective-permute-start | bytes 786440 | tf_op jit(solution)/shard_map/ppermute | solution.py:336
  18.7 9.0 %collective-permute-start.16 = (bf16[1024,128]{1,0:T(8,128)(2,1)}, bf16[1024,128]{1,0:T(8,128)(2,1)S(1)}, u32[]{:S(2)}, u32[]{:S(2)}) collective-permute-start(bf16[1024,128]{1,0:T(8,128)(2,1)} %get-tuple-element.67), channel_id=1, source_target_pairs={{0,4},{1,5},{2,6},{3,7},{4,0},{5,1},{6,2},{7,3},{8,12},{9,13},{10,... | collective-permute-start | bytes 786440 | tf_op jit(solution)/shard_map/ppermute | solution.py:336
  19.9 11.9 %collective-permute-start.17 = (bf16[1024,128]{1,0:T(8,128)(2,1)}, bf16[1024,128]{1,0:T(8,128)(2,1)S(1)}, u32[]{:S(2)}, u32[]{:S(2)}) collective-permute-start(bf16[1024,128]{1,0:T(8,128)(2,1)} %get-tuple-element.68), channel_id=1, source_target_pairs={{0,6},{1,7},{2,4},{3,5},{4,2},{5,3},{6,0},{7,1},{8,14},{9,15},{10,... | collective-permute-start | bytes 786440 | tf_op jit(solution)/shard_map/ppermute | solution.py:336
  20.0 16.5 %collective-permute-start.21 = (bf16[1024,128]{1,0:T(8,128)(2,1)}, bf16[1024,128]{1,0:T(8,128)(2,1)S(1)}, u32[]{:S(2)}, u32[]{:S(2)}) collective-permute-start(bf16[1024,128]{1,0:T(8,128)(2,1)} %get-tuple-element.74), channel_id=1, source_target_pairs={{0,2},{1,3},{2,0},{3,1},{4,6},{5,7},{6,4},{7,5},{8,10},{9,11},{10,... | collective-permute-start | bytes 786440 | tf_op jit(solution)/shard_map/ppermute | solution.py:336
  26.2 16.1 %collective-permute-start.3 = (bf16[1040,128]{1,0:T(8,128)(2,1)}, bf16[1040,128]{1,0:T(8,128)(2,1)S(1)}, u32[]{:S(2)}, u32[]{:S(2)}) collective-permute-start(bf16[1040,128]{1,0:T(8,128)(2,1)} %get-tuple-element.48), channel_id=1, source_target_pairs={{0,2},{1,3},{2,0},{3,1},{4,6},{5,7},{6,4},{7,5},{8,10},{9,11},{10,... | collective-permute-start | bytes 798728 | tf_op jit(solution)/shard_map/ppermute | solution.py:336
  26.3 39.2 %copy-start.5 = (bf16[1024,128]{1,0:T(8,128)(2,1)}, bf16[1024,128]{1,0:T(8,128)(2,1)S(1)}, u32[]{:S(2)}) copy-start(bf16[1024,128]{1,0:T(8,128)(2,1)S(1)} %collective-permute-done.15.refs_1_) | copy-start | bytes 786436
  26.3 17.1 %collective-permute-start.4 = (bf16[1040,128]{1,0:T(8,128)(2,1)}, bf16[1040,128]{1,0:T(8,128)(2,1)S(1)}, u32[]{:S(2)}, u32[]{:S(2)}) collective-permute-start(bf16[1040,128]{1,0:T(8,128)(2,1)} %get-tuple-element.49), channel_id=1, source_target_pairs={{0,4},{1,5},{2,6},{3,7},{4,0},{5,1},{6,2},{7,3},{8,12},{9,13},{10,... | collective-permute-start | bytes 798728 | tf_op jit(solution)/shard_map/ppermute | solution.py:336
  27.7 37.8 %copy-start.6 = (bf16[1024,128]{1,0:T(8,128)(2,1)}, bf16[1024,128]{1,0:T(8,128)(2,1)S(1)}, u32[]{:S(2)}) copy-start(bf16[1024,128]{1,0:T(8,128)(2,1)S(1)} %collective-permute-done.16.refs_2_) | copy-start | bytes 786436
  27.7 21.2 %collective-permute-start.5 = (bf16[1040,128]{1,0:T(8,128)(2,1)}, bf16[1040,128]{1,0:T(8,128)(2,1)S(1)}, u32[]{:S(2)}, u32[]{:S(2)}) collective-permute-start(bf16[1040,128]{1,0:T(8,128)(2,1)} %get-tuple-element.50), channel_id=1, source_target_pairs={{0,6},{1,7},{2,4},{3,5},{4,2},{5,3},{6,0},{7,1},{8,14},{9,15},{10,... | collective-permute-start | bytes 798728 | tf_op jit(solution)/shard_map/ppermute | solution.py:336
  31.8 33.7 %copy-start.7 = (bf16[1024,128]{1,0:T(8,128)(2,1)}, bf16[1024,128]{1,0:T(8,128)(2,1)S(1)}, u32[]{:S(2)}) copy-start(bf16[1024,128]{1,0:T(8,128)(2,1)S(1)} %collective-permute-done.17.refs_3_) | copy-start | bytes 786436
  31.8 22.3 %collective-permute-start.22 = (bf16[1024,128]{1,0:T(8,128)(2,1)}, bf16[1024,128]{1,0:T(8,128)(2,1)S(1)}, u32[]{:S(2)}, u32[]{:S(2)}) collective-permute-start(bf16[1024,128]{1,0:T(8,128)(2,1)} %get-tuple-element.75), channel_id=1, source_target_pairs={{0,4},{1,5},{2,6},{3,7},{4,0},{5,1},{6,2},{7,3},{8,12},{9,13},{10,... | collective-permute-start | bytes 786440 | tf_op jit(solution)/shard_map/ppermute | solution.py:336
  36.5 26.1 %copy-start.9 = (bf16[1024,128]{1,0:T(8,128)(2,1)}, bf16[1024,128]{1,0:T(8,128)(2,1)S(1)}, u32[]{:S(2)}) copy-start(bf16[1024,128]{1,0:T(8,128)(2,1)S(1)} %collective-permute-done.21.refs_1_) | copy-start | bytes 786436
  36.5 19.0 %collective-permute-start.23 = (bf16[1024,128]{1,0:T(8,128)(2,1)}, bf16[1024,128]{1,0:T(8,128)(2,1)S(1)}, u32[]{:S(2)}, u32[]{:S(2)}) collective-permute-start(bf16[1024,128]{1,0:T(8,128)(2,1)} %get-tuple-element.76), channel_id=1, source_target_pairs={{0,6},{1,7},{2,4},{3,5},{4,2},{5,3},{6,0},{7,1},{8,14},{9,15},{10,... | collective-permute-start | bytes 786440 | tf_op jit(solution)/shard_map/ppermute | solution.py:336
  42.2 7.8 %copy-start.2 = (bf16[1040,128]{1,0:T(8,128)(2,1)}, bf16[1040,128]{1,0:T(8,128)(2,1)S(1)}, u32[]{:S(2)}) copy-start(bf16[1040,128]{1,0:T(8,128)(2,1)S(1)} %collective-permute-done.3.refs_1_) | copy-start | bytes 798724
  42.2 26.2 %collective-permute-start.9 = (bf16[1024,128]{1,0:T(8,128)(2,1)S(1)}, bf16[1024,128]{1,0:T(8,128)(2,1)S(1)}, u32[]{:S(2)}, u32[]{:S(2)}) collective-permute-start(bf16[1024,128]{1,0:T(8,128)(2,1)S(1)} %copy-done.33), channel_id=1, source_target_pairs={{0,2},{1,3},{2,0},{3,1},{4,6},{5,7},{6,4},{7,5},{8,10},{9,11},{10,... | collective-permute-start | bytes 786440 | tf_op jit(solution)/shard_map/ppermute | solution.py:336
  43.4 6.7 %copy-start.3 = (bf16[1040,128]{1,0:T(8,128)(2,1)}, bf16[1040,128]{1,0:T(8,128)(2,1)S(1)}, u32[]{:S(2)}) copy-start(bf16[1040,128]{1,0:T(8,128)(2,1)S(1)} %collective-permute-done.4.refs_2_) | copy-start | bytes 798724
  43.4 25.3 %collective-permute-start.10 = (bf16[1024,128]{1,0:T(8,128)(2,1)S(1)}, bf16[1024,128]{1,0:T(8,128)(2,1)S(1)}, u32[]{:S(2)}, u32[]{:S(2)}) collective-permute-start(bf16[1024,128]{1,0:T(8,128)(2,1)S(1)} %copy-done.32), channel_id=1, source_target_pairs={{0,4},{1,5},{2,6},{3,7},{4,0},{5,1},{6,2},{7,3},{8,12},{9,13},{10,... | collective-permute-start | bytes 786440 | tf_op jit(solution)/shard_map/ppermute | solution.py:336
  48.9 20.1 %collective-permute-start.11 = (bf16[1024,128]{1,0:T(8,128)(2,1)S(1)}, bf16[1024,128]{1,0:T(8,128)(2,1)S(1)}, u32[]{:S(2)}, u32[]{:S(2)}) collective-permute-start(bf16[1024,128]{1,0:T(8,128)(2,1)S(1)} %copy-done.31), channel_id=1, source_target_pairs={{0,6},{1,7},{2,4},{3,5},{4,2},{5,3},{6,0},{7,1},{8,14},{9,15},{10,... | collective-permute-start | bytes 786440 | tf_op jit(solution)/shard_map/ppermute | solution.py:336
  54.1 8.5 %copy-start.12 = (bf16[1024,128]{1,0:T(8,128)(2,1)}, bf16[1024,128]{1,0:T(8,128)(2,1)S(1)}, u32[]{:S(2)}) copy-start(bf16[1024,128]{1,0:T(8,128)(2,1)S(1)} %collective-permute-done.22.refs_2_) | copy-start | bytes 786436
  54.1 18.1 %collective-permute-start.6 = (bf16[512,128]{1,0:T(8,128)(2,1)}, bf16[512,128]{1,0:T(8,128)(2,1)S(1)}, u32[]{:S(2)}, u32[]{:S(2)}) collective-permute-start(bf16[512,128]{1,0:T(8,128)(2,1)} %get-tuple-element.52), channel_id=1, source_target_pairs={{0,8},{1,9},{2,10},{3,11},{4,12},{5,13},{6,14},{7,15},{8,0},{9,1},... | collective-permute-start | bytes 393224 | tf_op jit(solution)/shard_map/ppermute | solution.py:336
  55.5 7.1 %copy-start.13 = (bf16[1024,128]{1,0:T(8,128)(2,1)}, bf16[1024,128]{1,0:T(8,128)(2,1)S(1)}, u32[]{:S(2)}) copy-start(bf16[1024,128]{1,0:T(8,128)(2,1)S(1)} %collective-permute-done.23.refs_3_) | copy-start | bytes 786436
  55.5 16.9 %collective-permute-start.7 = (bf16[512,128]{1,0:T(8,128)(2,1)}, bf16[512,128]{1,0:T(8,128)(2,1)S(1)}, u32[]{:S(2)}, u32[]{:S(2)}) collective-permute-start(bf16[512,128]{1,0:T(8,128)(2,1)} %get-tuple-element.53), channel_id=1, source_target_pairs={{0,16},{1,17},{2,18},{3,19},{4,20},{5,21},{6,22},{7,23},{8,24},{9,... | collective-permute-start | bytes 393224 | tf_op jit(solution)/shard_map/ppermute | solution.py:336
  62.6 5.8 %copy-start.36 = (bf16[512,128]{1,0:T(8,128)(2,1)S(1)}, bf16[512,128]{1,0:T(8,128)(2,1)}, u32[]{:S(2)}) copy-start(bf16[512,128]{1,0:T(8,128)(2,1)} %get-tuple-element.54) | copy-start | bytes 393220
  65.5 3.2 %copy-start.39 = (bf16[512,128]{1,0:T(8,128)(2,1)S(1)}, bf16[512,128]{1,0:T(8,128)(2,1)}, u32[]{:S(2)}) copy-start(bf16[512,128]{1,0:T(8,128)(2,1)} %get-tuple-element.78) | copy-start | bytes 393220
  65.5 3.5 %copy-start.38 = (bf16[512,128]{1,0:T(8,128)(2,1)S(1)}, bf16[512,128]{1,0:T(8,128)(2,1)}, u32[]{:S(2)}) copy-start(bf16[512,128]{1,0:T(8,128)(2,1)} %get-tuple-element.79) | copy-start | bytes 393220
  65.5 6.7 %copy-start.37 = (bf16[512,128]{1,0:T(8,128)(2,1)S(1)}, bf16[512,128]{1,0:T(8,128)(2,1)}, u32[]{:S(2)}) copy-start(bf16[512,128]{1,0:T(8,128)(2,1)} %get-tuple-element.80) | copy-start | bytes 393220
  68.4 7.0 %copy-start.35 = (bf16[512,128]{1,0:T(8,128)(2,1)S(1)}, bf16[512,128]{1,0:T(8,128)(2,1)}, u32[]{:S(2)}) copy-start(bf16[512,128]{1,0:T(8,128)(2,1)} %get-tuple-element.71) | copy-start | bytes 393220
  68.4 10.3 %copy-start.34 = (bf16[512,128]{1,0:T(8,128)(2,1)S(1)}, bf16[512,128]{1,0:T(8,128)(2,1)}, u32[]{:S(2)}) copy-start(bf16[512,128]{1,0:T(8,128)(2,1)} %get-tuple-element.72) | copy-start | bytes 393220
  68.4 4.2 %copy-start.8 = (bf16[1024,128]{1,0:T(8,128)(2,1)}, bf16[1024,128]{1,0:T(8,128)(2,1)S(1)}, u32[]{:S(2)}) copy-start(bf16[1024,128]{1,0:T(8,128)(2,1)S(1)} %collective-permute-done.9.refs_1_) | copy-start | bytes 786436
  68.5 7.0 %collective-permute-start.8 = (bf16[512,128]{1,0:T(8,128)(2,1)S(1)}, bf16[512,128]{1,0:T(8,128)(2,1)S(1)}, u32[]{:S(2)}, u32[]{:S(2)}) collective-permute-start(bf16[512,128]{1,0:T(8,128)(2,1)S(1)} %copy-done.36), channel_id=1, source_target_pairs={{0,24},{1,25},{2,26},{3,27},{4,28},{5,29},{6,30},{7,31},{8,16},{9,... | collective-permute-start | bytes 393224 | tf_op jit(solution)/shard_map/ppermute | solution.py:336
  68.7 3.9 %copy-start.10 = (bf16[1024,128]{1,0:T(8,128)(2,1)}, bf16[1024,128]{1,0:T(8,128)(2,1)S(1)}, u32[]{:S(2)}) copy-start(bf16[1024,128]{1,0:T(8,128)(2,1)S(1)} %collective-permute-done.10.refs_2_) | copy-start | bytes 786436
  68.7 10.0 %collective-permute-start.24 = (bf16[512,128]{1,0:T(8,128)(2,1)S(1)}, bf16[512,128]{1,0:T(8,128)(2,1)S(1)}, u32[]{:S(2)}, u32[]{:S(2)}) collective-permute-start(bf16[512,128]{1,0:T(8,128)(2,1)S(1)} %copy-done.39), channel_id=1, source_target_pairs={{0,8},{1,9},{2,10},{3,11},{4,12},{5,13},{6,14},{7,15},{8,0},{9,1},... | collective-permute-start | bytes 393224 | tf_op jit(solution)/shard_map/ppermute | solution.py:336
  69.0 3.6 %copy-start.11 = (bf16[1024,128]{1,0:T(8,128)(2,1)}, bf16[1024,128]{1,0:T(8,128)(2,1)S(1)}, u32[]{:S(2)}) copy-start(bf16[1024,128]{1,0:T(8,128)(2,1)S(1)} %collective-permute-done.11.refs_3_) | copy-start | bytes 786436
  69.0 12.1 %collective-permute-start.25 = (bf16[512,128]{1,0:T(8,128)(2,1)S(1)}, bf16[512,128]{1,0:T(8,128)(2,1)S(1)}, u32[]{:S(2)}, u32[]{:S(2)}) collective-permute-start(bf16[512,128]{1,0:T(8,128)(2,1)S(1)} %copy-done.38), channel_id=1, source_target_pairs={{0,16},{1,17},{2,18},{3,19},{4,20},{5,21},{6,22},{7,23},{8,24},{9,... | collective-permute-start | bytes 393224 | tf_op jit(solution)/shard_map/ppermute | solution.py:336
  72.2 34.2 %copy-start.16 = (bf16[512,128]{1,0:T(8,128)(2,1)}, bf16[512,128]{1,0:T(8,128)(2,1)S(1)}, u32[]{:S(2)}) copy-start(bf16[512,128]{1,0:T(8,128)(2,1)S(1)} %collective-permute-done.6.refs_1_) | copy-start | bytes 393220
  72.2 8.9 %collective-permute-start.26 = (bf16[512,128]{1,0:T(8,128)(2,1)S(1)}, bf16[512,128]{1,0:T(8,128)(2,1)S(1)}, u32[]{:S(2)}, u32[]{:S(2)}) collective-permute-start(bf16[512,128]{1,0:T(8,128)(2,1)S(1)} %copy-done.37), channel_id=1, source_target_pairs={{0,24},{1,25},{2,26},{3,27},{4,28},{5,29},{6,30},{7,31},{8,16},{9,... | collective-permute-start | bytes 393224 | tf_op jit(solution)/shard_map/ppermute | solution.py:336
  72.4 33.9 %copy-start.17 = (bf16[512,128]{1,0:T(8,128)(2,1)}, bf16[512,128]{1,0:T(8,128)(2,1)S(1)}, u32[]{:S(2)}) copy-start(bf16[512,128]{1,0:T(8,128)(2,1)S(1)} %collective-permute-done.7.refs_2_) | copy-start | bytes 393220
  72.4 19.1 %collective-permute-start.18 = (bf16[512,128]{1,0:T(8,128)(2,1)}, bf16[512,128]{1,0:T(8,128)(2,1)S(1)}, u32[]{:S(2)}, u32[]{:S(2)}) collective-permute-start(bf16[512,128]{1,0:T(8,128)(2,1)} %get-tuple-element.70), channel_id=1, source_target_pairs={{0,8},{1,9},{2,10},{3,11},{4,12},{5,13},{6,14},{7,15},{8,0},{9,1},... | collective-permute-start | bytes 393224 | tf_op jit(solution)/shard_map/ppermute | solution.py:336
  75.4 31.0 %copy-start.18 = (bf16[512,128]{1,0:T(8,128)(2,1)}, bf16[512,128]{1,0:T(8,128)(2,1)S(1)}, u32[]{:S(2)}) copy-start(bf16[512,128]{1,0:T(8,128)(2,1)S(1)} %collective-permute-done.8.refs_3_) | copy-start | bytes 393220
  75.4 21.7 %collective-permute-start.19 = (bf16[512,128]{1,0:T(8,128)(2,1)S(1)}, bf16[512,128]{1,0:T(8,128)(2,1)S(1)}, u32[]{:S(2)}, u32[]{:S(2)}) collective-permute-start(bf16[512,128]{1,0:T(8,128)(2,1)S(1)} %copy-done.35), channel_id=1, source_target_pairs={{0,16},{1,17},{2,18},{3,19},{4,20},{5,21},{6,22},{7,23},{8,24},{9,... | collective-permute-start | bytes 393224 | tf_op jit(solution)/shard_map/ppermute | solution.py:336
  78.7 27.7 %copy-start.19 = (bf16[512,128]{1,0:T(8,128)(2,1)}, bf16[512,128]{1,0:T(8,128)(2,1)S(1)}, u32[]{:S(2)}) copy-start(bf16[512,128]{1,0:T(8,128)(2,1)S(1)} %collective-permute-done.24.refs_13_) | copy-start | bytes 393220
  78.7 18.4 %collective-permute-start.20 = (bf16[512,128]{1,0:T(8,128)(2,1)S(1)}, bf16[512,128]{1,0:T(8,128)(2,1)S(1)}, u32[]{:S(2)}, u32[]{:S(2)}) collective-permute-start(bf16[512,128]{1,0:T(8,128)(2,1)S(1)} %copy-done.34), channel_id=1, source_target_pairs={{0,24},{1,25},{2,26},{3,27},{4,28},{5,29},{6,30},{7,31},{8,16},{9,... | collective-permute-start | bytes 393224 | tf_op jit(solution)/shard_map/ppermute | solution.py:336
  81.1 25.3 %copy-start.20 = (bf16[512,128]{1,0:T(8,128)(2,1)}, bf16[512,128]{1,0:T(8,128)(2,1)S(1)}, u32[]{:S(2)}) copy-start(bf16[512,128]{1,0:T(8,128)(2,1)S(1)} %collective-permute-done.25.refs_14_) | copy-start | bytes 393220
  81.1 16.0 %collective-permute-start.12 = (bf16[512,128]{1,0:T(8,128)(2,1)}, bf16[512,128]{1,0:T(8,128)(2,1)S(1)}, u32[]{:S(2)}, u32[]{:S(2)}) collective-permute-start(bf16[512,128]{1,0:T(8,128)(2,1)} %get-tuple-element.62), channel_id=1, source_target_pairs={{0,8},{1,9},{2,10},{3,11},{4,12},{5,13},{6,14},{7,15},{8,0},{9,1},... | collective-permute-start | bytes 393224 | tf_op jit(solution)/shard_map/ppermute | solution.py:336
  81.1 25.3 %copy-start.21 = (bf16[512,128]{1,0:T(8,128)(2,1)}, bf16[512,128]{1,0:T(8,128)(2,1)S(1)}, u32[]{:S(2)}) copy-start(bf16[512,128]{1,0:T(8,128)(2,1)S(1)} %collective-permute-done.26.refs_15_) | copy-start | bytes 393220
  81.1 25.3 %collective-permute-start.13 = (bf16[512,128]{1,0:T(8,128)(2,1)}, bf16[512,128]{1,0:T(8,128)(2,1)S(1)}, u32[]{:S(2)}, u32[]{:S(2)}) collective-permute-start(bf16[512,128]{1,0:T(8,128)(2,1)} %get-tuple-element.63), channel_id=1, source_target_pairs={{0,16},{1,17},{2,18},{3,19},{4,20},{5,21},{6,22},{7,23},{8,24},{9,... | collective-permute-start | bytes 393224 | tf_op jit(solution)/shard_map/ppermute | solution.py:336
  91.5 14.9 %copy-start.22 = (bf16[512,128]{1,0:T(8,128)(2,1)}, bf16[512,128]{1,0:T(8,128)(2,1)S(1)}, u32[]{:S(2)}) copy-start(bf16[512,128]{1,0:T(8,128)(2,1)S(1)} %collective-permute-done.18.refs_9_) | copy-start | bytes 393220
  91.5 14.8 %collective-permute-start.14 = (bf16[512,128]{1,0:T(8,128)(2,1)}, bf16[512,128]{1,0:T(8,128)(2,1)S(1)}, u32[]{:S(2)}, u32[]{:S(2)}) collective-permute-start(bf16[512,128]{1,0:T(8,128)(2,1)} %get-tuple-element.64), channel_id=1, source_target_pairs={{0,24},{1,25},{2,26},{3,27},{4,28},{5,29},{6,30},{7,31},{8,16},{9,... | collective-permute-start | bytes 393224 | tf_op jit(solution)/shard_map/ppermute | solution.py:336
  97.1 9.3 %copy-start.23 = (bf16[512,128]{1,0:T(8,128)(2,1)}, bf16[512,128]{1,0:T(8,128)(2,1)S(1)}, u32[]{:S(2)}) copy-start(bf16[512,128]{1,0:T(8,128)(2,1)S(1)} %collective-permute-done.19.refs_10_) | copy-start | bytes 393220
  97.1 9.3 %copy-start.24 = (bf16[512,128]{1,0:T(8,128)(2,1)}, bf16[512,128]{1,0:T(8,128)(2,1)S(1)}, u32[]{:S(2)}) copy-start(bf16[512,128]{1,0:T(8,128)(2,1)S(1)} %collective-permute-done.20.refs_11_) | copy-start | bytes 393220
  97.1 9.3 %copy-start.25 = (bf16[512,128]{1,0:T(8,128)(2,1)}, bf16[512,128]{1,0:T(8,128)(2,1)S(1)}, u32[]{:S(2)}) copy-start(bf16[512,128]{1,0:T(8,128)(2,1)S(1)} %collective-permute-done.12.refs_5_) | copy-start | bytes 393220
  109.8 3.5 %collective-permute-start.27 = (bf16[2,64,512]{2,1,0:T(8,128)(2,1)}, bf16[2,64,512]{2,1,0:T(8,128)(2,1)S(1)}, u32[]{:S(2)}, u32[]{:S(2)}) collective-permute-start(bf16[2,64,512]{2,1,0:T(8,128)(2,1)} %bitcast.27), channel_id=1, source_target_pairs={{0,4},{4,8},{8,12},{12,16},{16,20},{20,24},{24,28},{1,5},{5,9},{9,... | collective-permute-start | bytes 393224 | tf_op jit(solution)/shard_map/ppermute | solution.py:453
  111.1 9.3 %collective-permute-start.28 = (bf16[2,64,512]{2,1,0:T(8,128)(2,1)}, bf16[2,64,512]{2,1,0:T(8,128)(2,1)S(1)}, u32[]{:S(2)}, u32[]{:S(2)}) collective-permute-start(bf16[2,64,512]{2,1,0:T(8,128)(2,1)} %bitcast.26), channel_id=1, source_target_pairs={{4,0},{8,4},{12,8},{16,12},{20,16},{24,20},{28,24},{5,1},{9,5},{13... | collective-permute-start | bytes 393224 | tf_op jit(solution)/shard_map/ppermute | solution.py:453
  113.4 18.0 %copy-start.14 = (bf16[2,64,512]{2,1,0:T(8,128)(2,1)}, bf16[2,64,512]{2,1,0:T(8,128)(2,1)S(1)}, u32[]{:S(2)}) copy-start(bf16[2,64,512]{2,1,0:T(8,128)(2,1)S(1)} %collective-permute-done.27.low_ref) | copy-start | bytes 393220
  120.4 11.0 %copy-start.15 = (bf16[2,64,512]{2,1,0:T(8,128)(2,1)}, bf16[2,64,512]{2,1,0:T(8,128)(2,1)S(1)}, u32[]{:S(2)}) copy-start(bf16[2,64,512]{2,1,0:T(8,128)(2,1)S(1)} %collective-permute-done.28.high_ref) | copy-start | bytes 393220
  120.5 8.3 %collective-permute-start.29 = (bf16[12,2,512]{2,1,0:T(2,128)(2,1)S(1)}, bf16[12,2,512]{2,1,0:T(2,128)(2,1)S(1)}, u32[]{:S(2)}, u32[]{:S(2)}) collective-permute-start(bf16[12,2,512]{2,1,0:T(2,128)(2,1)S(1)} %pad_maximum_fusion), channel_id=1, source_target_pairs={{0,1},{1,2},{2,3},{4,5},{5,6},{6,7},{8,9},{9,10},{10,11},{12,13},{... | collective-permute-start | bytes 73736 | tf_op jit(solution)/shard_map/ppermute | solution.py:453
  126.2 5.1 %collective-permute-start.30 = (bf16[12,2,512]{2,1,0:T(2,128)(2,1)S(1)}, bf16[12,2,512]{2,1,0:T(2,128)(2,1)S(1)}, u32[]{:S(2)}, u32[]{:S(2)}) collective-permute-start(bf16[12,2,512]{2,1,0:T(2,128)(2,1)S(1)} %pad_maximum_fusion.1), channel_id=1, source_target_pairs={{1,0},{2,1},{3,2},{5,4},{6,5},{7,6},{9,8},{10,9},{11,10},{13,12},{... | collective-permute-start | bytes 73736 | tf_op jit(solution)/shard_map/ppermute | solution.py:453
  (8 other events, 8.5 us)

commit v2 on v1

--- a/solution.py
+++ b/solution.py
@@ -6,6 +6,7 @@
 from jax.experimental import pallas as pl
 from jax.experimental.pallas import tpu as pltpu
 from jax.sharding import PartitionSpec as P
+
 
 DEPTH = 4
 TX = 8
@@ -14,7 +15,7 @@
 PARTS = (1, 1, 1, 1)
 LABEL_ROWS = 16
 VMEM = pltpu.VMEM
-LIMIT = 60 * 1024 * 1024
+LIMIT = 20 * 1024 * 1024
 
 
 def vmem():
@@ -175,8 +176,8 @@
         copy.start()
     else:
         plan_ref = refs[0]
-        outs = refs[2 : 2 + n_z]
-        (total,) = refs[2 + n_z :]
+        outs = refs[1 : 1 + n_z]
+        (total,) = refs[1 + n_z :]
     total[...] = jnp.zeros_like(total)
     if first:
         copy.wait()
@@ -207,7 +208,7 @@
 def finish_kernel(n_z, spans, blocks, size, *refs):
     count = n_z * len(spans)
     parts = refs[:count]
-    out_ref, low_ref, high_ref, total = refs[count:]
+    out_ref, low_ref, high_ref, total = refs[count + 1 :]
     for k, (start, chunk) in enumerate(spans):
         for block in range(blocks):
             row = block * chunk
@@ -227,7 +228,7 @@
         high_ref[:, lanes] = part[cells - 2 * TY :]
 
 
-def band_kernel(first_ref, second_ref, out1_ref, out2_ref):
+def band_kernel(first_ref, second_ref, after_ref, out1_ref, out2_ref):
     channels = first_ref.shape[-1]
     zero = jnp.zeros((channels, channels), jnp.bfloat16)
     for source, target in ((first_ref, out1_ref), (second_ref, out2_ref)):
@@ -385,7 +386,7 @@
             for g, value in enumerate(messages[k])
         ]
 
-    def merge(k, received, plan, after):
+    def merge(k, received, plan):
         first = k == 0
         chunk = spans[k][1]
         outs = arrays(n_z, blocks * chunk, channels)
@@ -402,8 +403,8 @@
                 pltpu.SemaphoreType.DMA,
             ]
         else:
-            in_specs += [smem(), anywhere()]
-            args += (plan, after)
+            in_specs.append(smem())
+            args += (plan,)
         return pl.pallas_call(
             functools.partial(merge_kernel, n_z, groups, slots, chunk, blocks, first),
             out_shape=tuple(outs),
@@ -413,24 +414,24 @@
             compiler_params=params(),
         )(*args)
 
-    bands = jax.ShapeDtypeStruct((3, 2, 9 * channels, 2 * channels), jnp.bfloat16)
-    band1, band2 = pl.pallas_call(
-        band_kernel,
-        out_shape=(bands, bands),
-        in_specs=[vmem(), vmem()],
-        out_specs=(vmem(), vmem()),
-        compiler_params=params(),
-        name="bands",
-    )(conv1_weight, conv2_weight)
     messages = {}
     contribute([0])
     contribute(list(range(1, len(spans))))
     plan, final = None, []
     for k in range(len(spans)):
-        merged = merge(k, exchange(k), plan, band1)
+        merged = merge(k, exchange(k), plan)
         if k == 0:
             plan = merged[-1]
         final += [moved_by(part, dz=dz) if dz else part for dz, part in enumerate(merged[:n_z])]
+    bands = jax.ShapeDtypeStruct((3, 2, 9 * channels, 2 * channels), jnp.bfloat16)
+    band1, band2 = pl.pallas_call(
+        band_kernel,
+        out_shape=(bands, bands),
+        in_specs=[vmem(), vmem(), anywhere()],
+        out_specs=(vmem(), vmem()),
+        compiler_params=params(),
+        name="bands",
+    )(conv1_weight, conv2_weight, merged[0])
     cells = TX * TY
     lanes = DEPTH * channels
     main, first_rows, last_rows = pl.pallas_call(
@@ -440,12 +441,12 @@
             jax.ShapeDtypeStruct((2 * TY, lanes), jnp.bfloat16),
             jax.ShapeDtypeStruct((2 * TY, lanes), jnp.bfloat16),
         ),
-        in_specs=[vmem()] * len(final),
+        in_specs=[vmem()] * len(final) + [anywhere()],
         out_specs=(vmem(),) * 3,
         scratch_shapes=[VMEM((cells * DEPTH, channels), jnp.float32)],
         compiler_params=params(),
         name="finish",
-    )(*final)
+    )(*final, band1)
     main = main.reshape(TX, TY, lanes)
 
     def moved(value, axis, count, step):

time: 143 us -> 128 us (0.90)
  Pallas kernels: 44.3 us -> 24.3 us
  starting transfers between devices: 47.4 us -> 53.6 us
    pallas_call x2, Pallas kernels: 11.3 us -> 5.78 us  [contribute(): pl.pallas_call(functools.partial(contribute_kernel, n_c, groups, per_grou...]
    pallas_call x4, Pallas kernels: 12.6 us -> 7.45 us  [merge(): pl.pallas_call(functools.partial(merge_kernel, n_z, groups, slots, chunk,...]
    pallas_call x1, Pallas kernels: 4.83 us -> 0.91 us  [shards(): pl.pallas_call(band_kernel, out_shape=(bands, bands), in_specs=[vmem(), v...]
    ppermute x27, starting transfers between devices: 37.2 us -> 40.4 us  [moved_by(): return lax.ppermute(value, ('frames', 'rows'), pairs)]
    ppermute x4, starting transfers between devices: 10.2 us -> 13.2 us  [moved(): return lax.ppermute(value, axis, pairs)]
    pallas_call x1, Pallas kernels: 10.2 us -> 7.4 us  [shards(): pl.pallas_call(convolve_kernel, out_shape=jax.ShapeDtypeStruct((cells * D...]
    pallas_call x1, Pallas kernels: 2.77 us -> 0.35 us  [shards(): pl.pallas_call(functools.partial(finish_kernel, n_z, spans, blocks, size)...]
    ppermute x4, waiting for transfers between devices: 9.68 us -> 7.66 us  [moved(): return lax.ppermute(value, axis, pairs)]
  transfers between devices with their start and end apart: 31 -> 31, of which waited for: 10 -> 13; matrix products, arithmetic and copies ran while one was open for 2% -> 1% of each run, Pallas kernels for 17% -> 10%
where the time goes in v2:
time: 128 us; the launch traced here: 126 us
  starting transfers between devices  53.6 us (42%)
  waiting for transfers between devices  42.8 us (33%)
  Pallas kernels  24.3 us (19%)
  local copies, waits for them, and re-layouts  4.02 us (3%)
    ppermute x27, starting transfers between devices, moved_by(): return lax.ppermute(value, ('frames', 'rows'), pairs)  40.4 us
    ppermute x27, waiting for transfers between devices, moved_by(): return lax.ppermute(value, ('frames', 'rows'), pairs)  35.1 us
    ppermute x4, starting transfers between devices, moved(): return lax.ppermute(value, axis, pairs)  13.2 us
    ppermute x4, waiting for transfers between devices, moved(): return lax.ppermute(value, axis, pairs)  7.66 us
    pallas_call x4, Pallas kernels, merge(): pl.pallas_call(functools.partial(merge_kernel, n_z, groups, slots, chunk,...  7.45 us
    pallas_call x1, Pallas kernels, shards(): pl.pallas_call(convolve_kernel, out_shape=jax.ShapeDtypeStruct((cells * D...  7.4 us
    pallas_call x2, Pallas kernels, contribute(): pl.pallas_call(functools.partial(contribute_kernel, n_c, groups, per_grou...  5.78 us
    unnamed x12, local copies, waits for them, and re-layouts  3.8 us
  transfers between devices with their start and end apart: 31, of which 13 were waited for; matrix products, arithmetic and copies ran while one was open for 1% of the time, Pallas kernels for 10%

profile of v2, /device:TPU:1, one launch (start us, length us, event | category | flops | bytes accessed | tf_op | source)
XLA Modules:
  0.0 126.0 jit_solution(6531646402690286879)
XLA Ops:
  0.0 0.0 collective-permute-start.1
  0.0 0.5 collective-permute-start.2
  0.5 0.7 multiply_add_fusion
  1.2 0.1 copy.10
  1.3 0.1 reshape.15.refs_1_
  1.4 0.1 collective-permute-start
  1.5 0.1 pad_add_fusion.refs_0_
  1.6 3.5 %collective-permute-done.refs_2_ = s32[64]{0:T(128)S(1)} collective-permute-done((s32[64]{0:T(128)S(1)}, s32[64]{0:T(128)S(1)}, u32[]{:S(2)}, u32[]{:S(2)}) %collective-permute-start) | collective-permute-done | bytes 288 | tf_op jit(solution)/shard_map/ppermute | solution.py:337
  5.1 2.5 %index.1 = (s32[128]{0:T(128)S(1)}, bf16[64,128]{1,0:T(8,128)(2,1)S(1)}) custom-call(s32[4]{0:T(128)S(1)} %pad_add_fusion.refs_0_, s32[64]{0:T(128)S(1)} %reshape.15.refs_1_, s32[64]{0:T(128)S(1)} %collective-permute-done.refs_2_), custom_call_target="tpu_custom_call" | custom-call | tf_op jit(solution)/shard_map/index/pallas_call | solution.py:346
  7.6 0.0 collective-permute-done.2.refs_4_
  7.6 0.0 copy-start
  7.6 1.6 %copy-done = bf16[1,16,4,128,128]{4,3,2,1,0:T(8,128)(2,1)S(1)} copy-done((bf16[1,16,4,128,128]{4,3,2,1,0:T(8,128)(2,1)S(1)}, bf16[1,16,4,128,128]{4,3,2,1,0:T(8,128)(2,1)}, u32[]{:S(2)}) %copy-start) | copy-done | bytes 2097176
  9.2 1.0 copy-done.1
  10.2 3.4 %shard_map.84 = (bf16[1024,128]{1,0:T(8,128)(2,1)S(1)}, bf16[1024,128]{1,0:T(8,128)(2,1)S(1)}, bf16[1024,128]{1,0:T(8,128)(2,1)S(1)}, bf16[1024,128]{1,0:T(8,128...) custom-call(s32[128]{0:T(128)S(1)} %get-tuple-element.45.refs_0_, ...), custom_call_target="tpu_custom_call" | custom-call | tf_op jit(solution)/shard_map/pallas_call | solution.py:372
  13.7 2.4 %collective-permute-start.9 = (bf16[1024,128]{1,0:T(8,128)(2,1)S(1)}, bf16[1024,128]{1,0:T(8,128)(2,1)S(1)}, u32[]{:S(2)}, u32[]{:S(2)}) collective-permute-start(bf16[1024,128]{1,0:T(8,128)(2,1)S(1)} %get-tuple-element.56), channel_id=1, source_target_pairs={{0,2},{1,3},{2,0},{3,1},{4,6},{5,7},{6,4},{7,5},{8,10},{9,11},{10,... | collective-permute-start | bytes 786440 | tf_op jit(solution)/shard_map/ppermute | solution.py:337
  16.1 1.2 collective-permute-start.10
  17.3 0.0 collective-permute-start.11
  17.3 1.4 %collective-permute-start.15 = (bf16[1024,128]{1,0:T(8,128)(2,1)S(1)}, bf16[1024,128]{1,0:T(8,128)(2,1)S(1)}, u32[]{:S(2)}, u32[]{:S(2)}) collective-permute-start(bf16[1024,128]{1,0:T(8,128)(2,1)S(1)} %get-tuple-element.65), channel_id=1, source_target_pairs={{0,2},{1,3},{2,0},{3,1},{4,6},{5,7},{6,4},{7,5},{8,10},{9,11},{10,... | collective-permute-start | bytes 786440 | tf_op jit(solution)/shard_map/ppermute | solution.py:337
  18.7 2.3 %shard_map.82 = (bf16[1040,128]{1,0:T(8,128)(2,1)S(1)}, bf16[1040,128]{1,0:T(8,128)(2,1)S(1)}, bf16[1040,128]{1,0:T(8,128)(2,1)S(1)}, bf16[1040,128]{1,0:T(8,128)(2,1)S(1)}) custom-call(s32[128]{0:T(128)S(1)} %get-tuple-element.45.refs_0_, bf16[64,128,128]{2,1,0:T(8,128)(2,1)S(1)} %bitcast.18, bf16[64,128,128]{2,1,0:T(8,128)(2,1)S(1)} %collective-permute-done.1.refs_2_, ...), custom_call_target="tpu_custom_call" | custom-call | tf_op jit(solution)/shard_map/pallas_call | solution.py:372
  21.1 0.1 collective-permute-start.3
  21.2 1.2 collective-permute-done.9.refs_1_
  22.4 1.2 collective-permute-start.4
  23.6 1.2 collective-permute-start.5
  24.8 4.2 %collective-permute-done.11.refs_3_ = bf16[1024,128]{1,0:T(8,128)(2,1)S(1)} collective-permute-done((bf16[1024,128]{1,0:T(8,128)(2,1)S(1)}, bf16[1024,128]{1,0:T(8,128)(2,1)S(1)}, u32[]{:S(2)}, u32[]{:S(2)}) %collective-permute-start.11) | collective-permute-done | bytes 262176 | tf_op jit(solution)/shard_map/ppermute | solution.py:337
  29.0 1.0 collective-permute-start.16
  29.9 3.7 %collective-permute-done.15.refs_1_ = bf16[1024,128]{1,0:T(8,128)(2,1)S(1)} collective-permute-done((bf16[1024,128]{1,0:T(8,128)(2,1)S(1)}, bf16[1024,128]{1,0:T(8,128)(2,1)S(1)}, u32[]{:S(2)}, u32[]{:S(2)}) %collective-permute-start.15) | collective-permute-done | bytes 262176 | tf_op jit(solution)/shard_map/ppermute | solution.py:337
  33.7 2.1 %collective-permute-start.17 = (bf16[1024,128]{1,0:T(8,128)(2,1)S(1)}, bf16[1024,128]{1,0:T(8,128)(2,1)S(1)}, u32[]{:S(2)}, u32[]{:S(2)}) collective-permute-start(bf16[1024,128]{1,0:T(8,128)(2,1)S(1)} %get-tuple-element.67), channel_id=1, source_target_pairs={{0,6},{1,7},{2,4},{3,5},{4,2},{5,3},{6,0},{7,1},{8,14},{9,15},{10,... | collective-permute-start | bytes 786440 | tf_op jit(solution)/shard_map/ppermute | solution.py:337
  35.8 3.6 %collective-permute-done.3.refs_1_ = bf16[1040,128]{1,0:T(8,128)(2,1)S(1)} collective-permute-done((bf16[1040,128]{1,0:T(8,128)(2,1)S(1)}, bf16[1040,128]{1,0:T(8,128)(2,1)S(1)}, u32[]{:S(2)}, u32[]{:S(2)}) %collective-permute-start.3) | collective-permute-done | bytes 266272 | tf_op jit(solution)/shard_map/ppermute | solution.py:337
  39.4 1.2 collective-permute-start.21
  40.6 1.2 collective-permute-start.22
  41.8 4.2 %collective-permute-done.5.refs_3_ = bf16[1040,128]{1,0:T(8,128)(2,1)S(1)} collective-permute-done((bf16[1040,128]{1,0:T(8,128)(2,1)S(1)}, bf16[1040,128]{1,0:T(8,128)(2,1)S(1)}, u32[]{:S(2)}, u32[]{:S(2)}) %collective-permute-start.5) | collective-permute-done | bytes 266272 | tf_op jit(solution)/shard_map/ppermute | solution.py:337
  46.0 1.2 collective-permute-start.23
  47.2 2.6 %shard_map.83 = (bf16[512,128]{1,0:T(8,128)(2,1)S(1)}, bf16[512,128]{1,0:T(8,128)(2,1)S(1)}, bf16[512,128]{1,0:T(8,128)(2,1)S(1)}, bf16[512,128]{1,0:T(8,128)(2,1)S(1)}, s32[132]{0:T(256)S(1)}) custom-call(bf16[1040,128]{1,0:T(8,128)(2,1)S(1)} %get-tuple-element.47.refs_0_, bf16[1040,128]{1,0:T(8,128)(2,1)S(1)} %collective-permute-done.3.refs_1_, ...), custom_call_target="tpu_custom_call" | custom-call | tf_op jit(solution)/shard_map/pallas_call | solution.py:408
  49.8 1.4 %collective-permute-start.6 = (bf16[512,128]{1,0:T(8,128)(2,1)S(1)}, bf16[512,128]{1,0:T(8,128)(2,1)S(1)}, u32[]{:S(2)}, u32[]{:S(2)}) collective-permute-start(bf16[512,128]{1,0:T(8,128)(2,1)S(1)} %get-tuple-element.52), channel_id=1, source_target_pairs={{0,8},{1,9},{2,10},{3,11},{4,12},{5,13},{6,14},{7,15},{8,0},{9,1},... | collective-permute-start | bytes 393224 | tf_op jit(solution)/shard_map/ppermute | solution.py:337
  51.2 0.5 collective-permute-done.17.refs_3_
  51.7 2.3 %collective-permute-start.7 = (bf16[512,128]{1,0:T(8,128)(2,1)S(1)}, bf16[512,128]{1,0:T(8,128)(2,1)S(1)}, u32[]{:S(2)}, u32[]{:S(2)}) collective-permute-start(bf16[512,128]{1,0:T(8,128)(2,1)S(1)} %get-tuple-element.53), channel_id=1, source_target_pairs={{0,16},{1,17},{2,18},{3,19},{4,20},{5,21},{6,22},{7,23},{8,24},{9,... | collective-permute-start | bytes 393224 | tf_op jit(solution)/shard_map/ppermute | solution.py:337
  54.0 1.4 %shard_map.85 = (bf16[512,128]{1,0:T(8,128)(2,1)S(1)}, bf16[512,128]{1,0:T(8,128)(2,1)S(1)}, bf16[512,128]{1,0:T(8,128)(2,1)S(1)}, bf16[512,128]{1,0:T(8,128)(2,1)S(1)}) custom-call(bf16[1024,128]{1,0:T(8,128)(2,1)S(1)} %get-tuple-element.55.refs_0_, bf16[1024,128]{1,0:T(8,128)(2,1)S(1)} %collective-permute-done.9.refs_1_, ...), custom_call_target="tpu_custom_call" | custom-call | tf_op jit(solution)/shard_map/pallas_call | solution.py:408
  55.4 1.4 %shard_map.86 = (bf16[512,128]{1,0:T(8,128)(2,1)S(1)}, bf16[512,128]{1,0:T(8,128)(2,1)S(1)}, bf16[512,128]{1,0:T(8,128)(2,1)S(1)}, bf16[512,128]{1,0:T(8,128)(2,1)S(1)}) custom-call(bf16[1024,128]{1,0:T(8,128)(2,1)S(1)} %get-tuple-element.64.refs_0_, bf16[1024,128]{1,0:T(8,128)(2,1)S(1)} %collective-permute-done.15.refs_1_, ...), custom_call_target="tpu_custom_call" | custom-call | tf_op jit(solution)/shard_map/pallas_call | solution.py:408
  56.8 2.8 %collective-permute-start.8 = (bf16[512,128]{1,0:T(8,128)(2,1)S(1)}, bf16[512,128]{1,0:T(8,128)(2,1)S(1)}, u32[]{:S(2)}, u32[]{:S(2)}) collective-permute-start(bf16[512,128]{1,0:T(8,128)(2,1)S(1)} %get-tuple-element.54), channel_id=1, source_target_pairs={{0,24},{1,25},{2,26},{3,27},{4,28},{5,29},{6,30},{7,31},{8,16},{9,... | collective-permute-start | bytes 393224 | tf_op jit(solution)/shard_map/ppermute | solution.py:337
  59.7 0.6 collective-permute-start.12
  60.3 2.6 %collective-permute-done.23.refs_3_ = bf16[1024,128]{1,0:T(8,128)(2,1)S(1)} collective-permute-done((bf16[1024,128]{1,0:T(8,128)(2,1)S(1)}, bf16[1024,128]{1,0:T(8,128)(2,1)S(1)}, u32[]{:S(2)}, u32[]{:S(2)}) %collective-permute-start.23) | collective-permute-done | bytes 262176 | tf_op jit(solution)/shard_map/ppermute | solution.py:337
  62.9 2.3 %collective-permute-start.13 = (bf16[512,128]{1,0:T(8,128)(2,1)S(1)}, bf16[512,128]{1,0:T(8,128)(2,1)S(1)}, u32[]{:S(2)}, u32[]{:S(2)}) collective-permute-start(bf16[512,128]{1,0:T(8,128)(2,1)S(1)} %get-tuple-element.62), channel_id=1, source_target_pairs={{0,16},{1,17},{2,18},{3,19},{4,20},{5,21},{6,22},{7,23},{8,24},{9,... | collective-permute-start | bytes 393224 | tf_op jit(solution)/shard_map/ppermute | solution.py:337
  65.3 1.1 collective-permute-start.14
  66.3 0.3 collective-permute-start.18
  66.6 2.0 %shard_map.87 = (bf16[512,128]{1,0:T(8,128)(2,1)S(1)}, bf16[512,128]{1,0:T(8,128)(2,1)}, bf16[512,128]{1,0:T(8,128)(2,1)S(1)}, bf16[512,128]{1,0:T(8,128)(2,1)S(1)}) custom-call(bf16[1024,128]{1,0:T(8,128)(2,1)S(1)} %get-tuple-element.72.refs_0_, bf16[1024,128]{1,0:T(8,128)(2,1)S(1)} %collective-permute-done.21.refs_1_, ...), custom_call_target="tpu_custom_call" | custom-call | tf_op jit(solution)/shard_map/pallas_call | solution.py:408
  68.7 2.2 %collective-permute-start.19 = (bf16[512,128]{1,0:T(8,128)(2,1)S(1)}, bf16[512,128]{1,0:T(8,128)(2,1)S(1)}, u32[]{:S(2)}, u32[]{:S(2)}) collective-permute-start(bf16[512,128]{1,0:T(8,128)(2,1)S(1)} %get-tuple-element.70), channel_id=1, source_target_pairs={{0,16},{1,17},{2,18},{3,19},{4,20},{5,21},{6,22},{7,23},{8,24},{9,... | collective-permute-start | bytes 393224 | tf_op jit(solution)/shard_map/ppermute | solution.py:337
  70.9 1.1 collective-permute-start.20
  71.9 0.7 collective-permute-start.24
  72.6 10.8 %collective-permute-start.25 = (bf16[512,128]{1,0:T(8,128)(2,1)S(1)}, bf16[512,128]{1,0:T(8,128)(2,1)S(1)}, u32[]{:S(2)}, u32[]{:S(2)}) collective-permute-start(bf16[512,128]{1,0:T(8,128)(2,1)S(1)} %get-tuple-element.78), channel_id=1, source_target_pairs={{0,16},{1,17},{2,18},{3,19},{4,20},{5,21},{6,22},{7,23},{8,24},{9,... | collective-permute-start | bytes 393224 | tf_op jit(solution)/shard_map/ppermute | solution.py:337
  83.4 0.0 copy-start.3
  83.5 1.2 copy-done.3
  84.6 0.9 bands.1
  85.5 1.7 %collective-permute-done.19.refs_10_ = bf16[512,128]{1,0:T(8,128)(2,1)S(1)} collective-permute-done((bf16[512,128]{1,0:T(8,128)(2,1)S(1)}, bf16[512,128]{1,0:T(8,128)(2,1)S(1)}, u32[]{:S(2)}, u32[]{:S(2)}) %collective-permute-start.19) | collective-permute-done | bytes 131104 | tf_op jit(solution)/shard_map/ppermute | solution.py:337
  87.2 9.8 %collective-permute-done.25.refs_14_ = bf16[512,128]{1,0:T(8,128)(2,1)S(1)} collective-permute-done((bf16[512,128]{1,0:T(8,128)(2,1)S(1)}, bf16[512,128]{1,0:T(8,128)(2,1)S(1)}, u32[]{:S(2)}, u32[]{:S(2)}) %collective-permute-start.25) | collective-permute-done | bytes 131104 | tf_op jit(solution)/shard_map/ppermute | solution.py:337
  97.1 0.3 finish.1
  97.4 4.6 %collective-permute-start.27 = (bf16[2,64,512]{2,1,0:T(8,128)(2,1)S(1)}, bf16[2,64,512]{2,1,0:T(8,128)(2,1)S(1)}, u32[]{:S(2)}, u32[]{:S(2)}) collective-permute-start(bf16[2,64,512]{2,1,0:T(8,128)(2,1)S(1)} %bitcast.27), channel_id=1, source_target_pairs={{0,4},{4,8},{8,12},{12,16},{16,20},{20,24},{24,28},{1,5},{5,9},{9,... | collective-permute-start | bytes 393224 | tf_op jit(solution)/shard_map/ppermute | solution.py:454
  102.0 1.3 %collective-permute-start.28 = (bf16[2,64,512]{2,1,0:T(8,128)(2,1)S(1)}, bf16[2,64,512]{2,1,0:T(8,128)(2,1)S(1)}, u32[]{:S(2)}, u32[]{:S(2)}) collective-permute-start(bf16[2,64,512]{2,1,0:T(8,128)(2,1)S(1)} %bitcast.26), channel_id=1, source_target_pairs={{4,0},{8,4},{12,8},{16,12},{20,16},{24,20},{28,24},{5,1},{9,5},{13... | collective-permute-start | bytes 393224 | tf_op jit(solution)/shard_map/ppermute | solution.py:454
  103.3 0.6 collective-permute-done.27.low_ref
  103.9 3.9 %collective-permute-done.28.high_ref = bf16[2,64,512]{2,1,0:T(8,128)(2,1)S(1)} collective-permute-done((bf16[2,64,512]{2,1,0:T(8,128)(2,1)S(1)}, bf16[2,64,512]{2,1,0:T(8,128)(2,1)S(1)}, u32[]{:S(2)}, u32[]{:S(2)}) %collective-permute-start.28) | collective-permute-done | bytes 131104 | tf_op jit(solution)/shard_map/ppermute | solution.py:454
  107.9 5.4 %collective-permute-start.29 = (bf16[12,2,512]{2,1,0:T(2,128)(2,1)S(1)}, bf16[12,2,512]{2,1,0:T(2,128)(2,1)S(1)}, u32[]{:S(2)}, u32[]{:S(2)}) collective-permute-start(bf16[12,2,512]{2,1,0:T(2,128)(2,1)S(1)} %pad_maximum_fusion), channel_id=1, source_target_pairs={{0,1},{1,2},{2,3},{4,5},{5,6},{6,7},{8,9},{9,10},{10,11},{12,13},{... | collective-permute-start | bytes 73736 | tf_op jit(solution)/shard_map/ppermute | solution.py:454
  113.4 1.9 %collective-permute-start.30 = (bf16[12,2,512]{2,1,0:T(2,128)(2,1)S(1)}, bf16[12,2,512]{2,1,0:T(2,128)(2,1)S(1)}, u32[]{:S(2)}, u32[]{:S(2)}) collective-permute-start(bf16[12,2,512]{2,1,0:T(2,128)(2,1)S(1)} %pad_maximum_fusion.1), channel_id=1, source_target_pairs={{1,0},{2,1},{3,2},{5,4},{6,5},{7,6},{9,8},{10,9},{11,10},{13,12},{... | collective-permute-start | bytes 73736 | tf_op jit(solution)/shard_map/ppermute | solution.py:454
  115.4 0.1 add_convert_fusion.ends_ref
  115.5 3.1 %collective-permute-done.30.right_ref = bf16[12,2,512]{2,1,0:T(2,128)(2,1)S(1)} collective-permute-done((bf16[12,2,512]{2,1,0:T(2,128)(2,1)S(1)}, bf16[12,2,512]{2,1,0:T(2,128)(2,1)S(1)}, u32[]{:S(2)}, u32[]{:S(2)}) %collective-permute-start.30) | collective-permute-done | bytes 24608 | tf_op jit(solution)/shard_map/ppermute | solution.py:454
  118.6 7.4 %convolve.1 = bf16[2048,128]{1,0:T(8,128)(2,1)} custom-call(s32[4]{0:T(128)S(1)} %add_convert_fusion.ends_ref, bf16[8,64,512]{2,1,0:T(8,128)(2,1)S(1)} %bitcast.23, bf16[2,64,512]{2,1,0:T(8,128)(2,1)S(1)} %collective-permute-done.27.low_ref, bf16[2,64,512]{2,1,0:T(8,128)(2,1)S(1)} %collective-permute-done.28.high_ref, ...), custom_call_target="tpu_custom_call" | custom-call | tf_op jit(solution)/shard_map/convolve/pallas_call | solution.py:464
  (30 shorter events, 0.2 us)
Async XLA Ops:
  0.0 7.6 %collective-permute-start.1 = (bf16[64,128,128]{2,1,0:T(8,128)(2,1)}, bf16[64,128,128]{2,1,0:T(8,128)(2,1)S(1)}, u32[]{:S(2)}, u32[]{:S(2)}) collective-permute-start(bf16[64,128,128]{2,1,0:T(8,128)(2,1)} %bitcast.16), channel_id=1, source_target_pairs={{0,1},{1,0},{2,3},{3,2},{4,5},{5,4},{6,7},{7,6},{8,9},{9,8},{10,11... | collective-permute-start | bytes 6291464 | tf_op jit(solution)/shard_map/ppermute | solution.py:337
  0.0 7.6 %collective-permute-start.2 = (bf16[16,128,128]{2,1,0:T(8,128)(2,1)}, bf16[16,128,128]{2,1,0:T(8,128)(2,1)S(1)}, u32[]{:S(2)}, u32[]{:S(2)}) collective-permute-start(bf16[16,128,128]{2,1,0:T(8,128)(2,1)} %bitcast.19), channel_id=1, source_target_pairs={{0,1},{1,0},{2,3},{3,2},{4,5},{5,4},{6,7},{7,6},{8,9},{9,8},{10,11... | collective-permute-start | bytes 1572872 | tf_op jit(solution)/shard_map/ppermute | solution.py:337
  1.4 3.7 %collective-permute-start = (s32[64]{0:T(128)S(1)}, s32[64]{0:T(128)S(1)}, u32[]{:S(2)}, u32[]{:S(2)}) collective-permute-start(s32[64]{0:T(128)S(1)} %reshape.15.refs_1_), channel_id=1, source_target_pairs={{0,1},{1,0},{2,3},{3,2},{4,5},{5,4},{6,7},{7,6},{8,9},{9,8},{10,11... | collective-permute-start | bytes 776 | tf_op jit(solution)/shard_map/ppermute | solution.py:337
  7.6 1.6 %copy-start = (bf16[1,16,4,128,128]{4,3,2,1,0:T(8,128)(2,1)S(1)}, bf16[1,16,4,128,128]{4,3,2,1,0:T(8,128)(2,1)}, u32[]{:S(2)}) copy-start(bf16[1,16,4,128,128]{4,3,2,1,0:T(8,128)(2,1)} %param.9) | copy-start | bytes 6291460
  9.2 1.0 copy-start.1
  13.7 8.7 %collective-permute-start.9 = (bf16[1024,128]{1,0:T(8,128)(2,1)S(1)}, bf16[1024,128]{1,0:T(8,128)(2,1)S(1)}, u32[]{:S(2)}, u32[]{:S(2)}) collective-permute-start(bf16[1024,128]{1,0:T(8,128)(2,1)S(1)} %get-tuple-element.56), channel_id=1, source_target_pairs={{0,2},{1,3},{2,0},{3,1},{4,6},{5,7},{6,4},{7,5},{8,10},{9,11},{10,... | collective-permute-start | bytes 786440 | tf_op jit(solution)/shard_map/ppermute | solution.py:337
  16.1 7.5 %collective-permute-start.10 = (bf16[1024,128]{1,0:T(8,128)(2,1)S(1)}, bf16[1024,128]{1,0:T(8,128)(2,1)S(1)}, u32[]{:S(2)}, u32[]{:S(2)}) collective-permute-start(bf16[1024,128]{1,0:T(8,128)(2,1)S(1)} %get-tuple-element.57), channel_id=1, source_target_pairs={{0,4},{1,5},{2,6},{3,7},{4,0},{5,1},{6,2},{7,3},{8,12},{9,13},{10,... | collective-permute-start | bytes 786440 | tf_op jit(solution)/shard_map/ppermute | solution.py:337
  17.3 11.7 %collective-permute-start.11 = (bf16[1024,128]{1,0:T(8,128)(2,1)S(1)}, bf16[1024,128]{1,0:T(8,128)(2,1)S(1)}, u32[]{:S(2)}, u32[]{:S(2)}) collective-permute-start(bf16[1024,128]{1,0:T(8,128)(2,1)S(1)} %get-tuple-element.58), channel_id=1, source_target_pairs={{0,6},{1,7},{2,4},{3,5},{4,2},{5,3},{6,0},{7,1},{8,14},{9,15},{10,... | collective-permute-start | bytes 786440 | tf_op jit(solution)/shard_map/ppermute | solution.py:337
  17.3 66.1 %copy-start.2 = (bf16[3,3,3,128,128]{4,3,2,1,0:T(8,128)(2,1)S(1)}, bf16[3,3,3,128,128]{4,3,2,1,0:T(8,128)(2,1)}, u32[]{:S(2)}) copy-start(bf16[3,3,3,128,128]{4,3,2,1,0:T(8,128)(2,1)} %first_ref.1) | copy-start | bytes 2654212
  17.3 16.3 %collective-permute-start.15 = (bf16[1024,128]{1,0:T(8,128)(2,1)S(1)}, bf16[1024,128]{1,0:T(8,128)(2,1)S(1)}, u32[]{:S(2)}, u32[]{:S(2)}) collective-permute-start(bf16[1024,128]{1,0:T(8,128)(2,1)S(1)} %get-tuple-element.65), channel_id=1, source_target_pairs={{0,2},{1,3},{2,0},{3,1},{4,6},{5,7},{6,4},{7,5},{8,10},{9,11},{10,... | collective-permute-start | bytes 786440 | tf_op jit(solution)/shard_map/ppermute | solution.py:337
  21.1 18.3 %collective-permute-start.3 = (bf16[1040,128]{1,0:T(8,128)(2,1)S(1)}, bf16[1040,128]{1,0:T(8,128)(2,1)S(1)}, u32[]{:S(2)}, u32[]{:S(2)}) collective-permute-start(bf16[1040,128]{1,0:T(8,128)(2,1)S(1)} %get-tuple-element.48), channel_id=1, source_target_pairs={{0,2},{1,3},{2,0},{3,1},{4,6},{5,7},{6,4},{7,5},{8,10},{9,11},{10,... | collective-permute-start | bytes 798728 | tf_op jit(solution)/shard_map/ppermute | solution.py:337
  22.4 18.2 %collective-permute-start.4 = (bf16[1040,128]{1,0:T(8,128)(2,1)S(1)}, bf16[1040,128]{1,0:T(8,128)(2,1)S(1)}, u32[]{:S(2)}, u32[]{:S(2)}) collective-permute-start(bf16[1040,128]{1,0:T(8,128)(2,1)S(1)} %get-tuple-element.49), channel_id=1, source_target_pairs={{0,4},{1,5},{2,6},{3,7},{4,0},{5,1},{6,2},{7,3},{8,12},{9,13},{10,... | collective-permute-start | bytes 798728 | tf_op jit(solution)/shard_map/ppermute | solution.py:337
  23.6 22.4 %collective-permute-start.5 = (bf16[1040,128]{1,0:T(8,128)(2,1)S(1)}, bf16[1040,128]{1,0:T(8,128)(2,1)S(1)}, u32[]{:S(2)}, u32[]{:S(2)}) collective-permute-start(bf16[1040,128]{1,0:T(8,128)(2,1)S(1)} %get-tuple-element.50), channel_id=1, source_target_pairs={{0,6},{1,7},{2,4},{3,5},{4,2},{5,3},{6,0},{7,1},{8,14},{9,15},{10,... | collective-permute-start | bytes 798728 | tf_op jit(solution)/shard_map/ppermute | solution.py:337
  29.0 20.8 %collective-permute-start.16 = (bf16[1024,128]{1,0:T(8,128)(2,1)S(1)}, bf16[1024,128]{1,0:T(8,128)(2,1)S(1)}, u32[]{:S(2)}, u32[]{:S(2)}) collective-permute-start(bf16[1024,128]{1,0:T(8,128)(2,1)S(1)} %get-tuple-element.66), channel_id=1, source_target_pairs={{0,4},{1,5},{2,6},{3,7},{4,0},{5,1},{6,2},{7,3},{8,12},{9,13},{10,... | collective-permute-start | bytes 786440 | tf_op jit(solution)/shard_map/ppermute | solution.py:337
  33.7 18.0 %collective-permute-start.17 = (bf16[1024,128]{1,0:T(8,128)(2,1)S(1)}, bf16[1024,128]{1,0:T(8,128)(2,1)S(1)}, u32[]{:S(2)}, u32[]{:S(2)}) collective-permute-start(bf16[1024,128]{1,0:T(8,128)(2,1)S(1)} %get-tuple-element.67), channel_id=1, source_target_pairs={{0,6},{1,7},{2,4},{3,5},{4,2},{5,3},{6,0},{7,1},{8,14},{9,15},{10,... | collective-permute-start | bytes 786440 | tf_op jit(solution)/shard_map/ppermute | solution.py:337
  39.4 17.4 %collective-permute-start.21 = (bf16[1024,128]{1,0:T(8,128)(2,1)S(1)}, bf16[1024,128]{1,0:T(8,128)(2,1)S(1)}, u32[]{:S(2)}, u32[]{:S(2)}) collective-permute-start(bf16[1024,128]{1,0:T(8,128)(2,1)S(1)} %get-tuple-element.73), channel_id=1, source_target_pairs={{0,2},{1,3},{2,0},{3,1},{4,6},{5,7},{6,4},{7,5},{8,10},{9,11},{10,... | collective-permute-start | bytes 786440 | tf_op jit(solution)/shard_map/ppermute | solution.py:337
  40.6 19.1 %collective-permute-start.22 = (bf16[1024,128]{1,0:T(8,128)(2,1)S(1)}, bf16[1024,128]{1,0:T(8,128)(2,1)S(1)}, u32[]{:S(2)}, u32[]{:S(2)}) collective-permute-start(bf16[1024,128]{1,0:T(8,128)(2,1)S(1)} %get-tuple-element.74), channel_id=1, source_target_pairs={{0,4},{1,5},{2,6},{3,7},{4,0},{5,1},{6,2},{7,3},{8,12},{9,13},{10,... | collective-permute-start | bytes 786440 | tf_op jit(solution)/shard_map/ppermute | solution.py:337
  46.0 16.9 %collective-permute-start.23 = (bf16[1024,128]{1,0:T(8,128)(2,1)S(1)}, bf16[1024,128]{1,0:T(8,128)(2,1)S(1)}, u32[]{:S(2)}, u32[]{:S(2)}) collective-permute-start(bf16[1024,128]{1,0:T(8,128)(2,1)S(1)} %get-tuple-element.75), channel_id=1, source_target_pairs={{0,6},{1,7},{2,4},{3,5},{4,2},{5,3},{6,0},{7,1},{8,14},{9,15},{10,... | collective-permute-start | bytes 786440 | tf_op jit(solution)/shard_map/ppermute | solution.py:337
  49.8 15.4 %collective-permute-start.6 = (bf16[512,128]{1,0:T(8,128)(2,1)S(1)}, bf16[512,128]{1,0:T(8,128)(2,1)S(1)}, u32[]{:S(2)}, u32[]{:S(2)}) collective-permute-start(bf16[512,128]{1,0:T(8,128)(2,1)S(1)} %get-tuple-element.52), channel_id=1, source_target_pairs={{0,8},{1,9},{2,10},{3,11},{4,12},{5,13},{6,14},{7,15},{8,0},{9,1},... | collective-permute-start | bytes 393224 | tf_op jit(solution)/shard_map/ppermute | solution.py:337
  51.7 14.7 %collective-permute-start.7 = (bf16[512,128]{1,0:T(8,128)(2,1)S(1)}, bf16[512,128]{1,0:T(8,128)(2,1)S(1)}, u32[]{:S(2)}, u32[]{:S(2)}) collective-permute-start(bf16[512,128]{1,0:T(8,128)(2,1)S(1)} %get-tuple-element.53), channel_id=1, source_target_pairs={{0,16},{1,17},{2,18},{3,19},{4,20},{5,21},{6,22},{7,23},{8,24},{9,... | collective-permute-start | bytes 393224 | tf_op jit(solution)/shard_map/ppermute | solution.py:337
  56.8 11.8 %collective-permute-start.8 = (bf16[512,128]{1,0:T(8,128)(2,1)S(1)}, bf16[512,128]{1,0:T(8,128)(2,1)S(1)}, u32[]{:S(2)}, u32[]{:S(2)}) collective-permute-start(bf16[512,128]{1,0:T(8,128)(2,1)S(1)} %get-tuple-element.54), channel_id=1, source_target_pairs={{0,24},{1,25},{2,26},{3,27},{4,28},{5,29},{6,30},{7,31},{8,16},{9,... | collective-permute-start | bytes 393224 | tf_op jit(solution)/shard_map/ppermute | solution.py:337
  59.7 11.2 %collective-permute-start.12 = (bf16[512,128]{1,0:T(8,128)(2,1)S(1)}, bf16[512,128]{1,0:T(8,128)(2,1)S(1)}, u32[]{:S(2)}, u32[]{:S(2)}) collective-permute-start(bf16[512,128]{1,0:T(8,128)(2,1)S(1)} %get-tuple-element.61), channel_id=1, source_target_pairs={{0,8},{1,9},{2,10},{3,11},{4,12},{5,13},{6,14},{7,15},{8,0},{9,1},... | collective-permute-start | bytes 393224 | tf_op jit(solution)/shard_map/ppermute | solution.py:337
  62.9 9.0 %collective-permute-start.13 = (bf16[512,128]{1,0:T(8,128)(2,1)S(1)}, bf16[512,128]{1,0:T(8,128)(2,1)S(1)}, u32[]{:S(2)}, u32[]{:S(2)}) collective-permute-start(bf16[512,128]{1,0:T(8,128)(2,1)S(1)} %get-tuple-element.62), channel_id=1, source_target_pairs={{0,16},{1,17},{2,18},{3,19},{4,20},{5,21},{6,22},{7,23},{8,24},{9,... | collective-permute-start | bytes 393224 | tf_op jit(solution)/shard_map/ppermute | solution.py:337
  65.3 7.3 %collective-permute-start.14 = (bf16[512,128]{1,0:T(8,128)(2,1)S(1)}, bf16[512,128]{1,0:T(8,128)(2,1)S(1)}, u32[]{:S(2)}, u32[]{:S(2)}) collective-permute-start(bf16[512,128]{1,0:T(8,128)(2,1)S(1)} %get-tuple-element.63), channel_id=1, source_target_pairs={{0,24},{1,25},{2,26},{3,27},{4,28},{5,29},{6,30},{7,31},{8,16},{9,... | collective-permute-start | bytes 393224 | tf_op jit(solution)/shard_map/ppermute | solution.py:337
  66.3 17.1 %collective-permute-start.18 = (bf16[512,128]{1,0:T(8,128)(2,1)S(1)}, bf16[512,128]{1,0:T(8,128)(2,1)S(1)}, u32[]{:S(2)}, u32[]{:S(2)}) collective-permute-start(bf16[512,128]{1,0:T(8,128)(2,1)S(1)} %get-tuple-element.69), channel_id=1, source_target_pairs={{0,8},{1,9},{2,10},{3,11},{4,12},{5,13},{6,14},{7,15},{8,0},{9,1},... | collective-permute-start | bytes 393224 | tf_op jit(solution)/shard_map/ppermute | solution.py:337
  68.7 18.6 %collective-permute-start.19 = (bf16[512,128]{1,0:T(8,128)(2,1)S(1)}, bf16[512,128]{1,0:T(8,128)(2,1)S(1)}, u32[]{:S(2)}, u32[]{:S(2)}) collective-permute-start(bf16[512,128]{1,0:T(8,128)(2,1)S(1)} %get-tuple-element.70), channel_id=1, source_target_pairs={{0,16},{1,17},{2,18},{3,19},{4,20},{5,21},{6,22},{7,23},{8,24},{9,... | collective-permute-start | bytes 393224 | tf_op jit(solution)/shard_map/ppermute | solution.py:337
  70.9 16.4 %collective-permute-start.20 = (bf16[512,128]{1,0:T(8,128)(2,1)S(1)}, bf16[512,128]{1,0:T(8,128)(2,1)S(1)}, u32[]{:S(2)}, u32[]{:S(2)}) collective-permute-start(bf16[512,128]{1,0:T(8,128)(2,1)S(1)} %get-tuple-element.71), channel_id=1, source_target_pairs={{0,24},{1,25},{2,26},{3,27},{4,28},{5,29},{6,30},{7,31},{8,16},{9,... | collective-permute-start | bytes 393224 | tf_op jit(solution)/shard_map/ppermute | solution.py:337
  71.9 15.3 %collective-permute-start.24 = (bf16[512,128]{1,0:T(8,128)(2,1)}, bf16[512,128]{1,0:T(8,128)(2,1)S(1)}, u32[]{:S(2)}, u32[]{:S(2)}) collective-permute-start(bf16[512,128]{1,0:T(8,128)(2,1)} %get-tuple-element.77), channel_id=1, source_target_pairs={{0,8},{1,9},{2,10},{3,11},{4,12},{5,13},{6,14},{7,15},{8,0},{9,1},... | collective-permute-start | bytes 393224 | tf_op jit(solution)/shard_map/ppermute | solution.py:337
  72.6 24.5 %collective-permute-start.25 = (bf16[512,128]{1,0:T(8,128)(2,1)S(1)}, bf16[512,128]{1,0:T(8,128)(2,1)S(1)}, u32[]{:S(2)}, u32[]{:S(2)}) collective-permute-start(bf16[512,128]{1,0:T(8,128)(2,1)S(1)} %get-tuple-element.78), channel_id=1, source_target_pairs={{0,16},{1,17},{2,18},{3,19},{4,20},{5,21},{6,22},{7,23},{8,24},{9,... | collective-permute-start | bytes 393224 | tf_op jit(solution)/shard_map/ppermute | solution.py:337
  83.4 13.6 %collective-permute-start.26 = (bf16[512,128]{1,0:T(8,128)(2,1)S(1)}, bf16[512,128]{1,0:T(8,128)(2,1)S(1)}, u32[]{:S(2)}, u32[]{:S(2)}) collective-permute-start(bf16[512,128]{1,0:T(8,128)(2,1)S(1)} %get-tuple-element.79), channel_id=1, source_target_pairs={{0,24},{1,25},{2,26},{3,27},{4,28},{5,29},{6,30},{7,31},{8,16},{9,... | collective-permute-start | bytes 393224 | tf_op jit(solution)/shard_map/ppermute | solution.py:337
  83.4 1.2 copy-start.3
  84.6 34.0 %copy-start.4 = (f32[128]{0:T(128)S(1)}, f32[128]{0:T(128)}, u32[]{:S(2)}) copy-start(f32[128]{0:T(128)} %param.13) | copy-start | bytes 1540
  84.6 34.0 %copy-start.5 = (f32[128]{0:T(128)S(1)}, f32[128]{0:T(128)}, u32[]{:S(2)}) copy-start(f32[128]{0:T(128)} %param.15) | copy-start | bytes 1540
  97.4 6.5 %collective-permute-start.27 = (bf16[2,64,512]{2,1,0:T(8,128)(2,1)S(1)}, bf16[2,64,512]{2,1,0:T(8,128)(2,1)S(1)}, u32[]{:S(2)}, u32[]{:S(2)}) collective-permute-start(bf16[2,64,512]{2,1,0:T(8,128)(2,1)S(1)} %bitcast.27), channel_id=1, source_target_pairs={{0,4},{4,8},{8,12},{12,16},{16,20},{20,24},{24,28},{1,5},{5,9},{9,... | collective-permute-start | bytes 393224 | tf_op jit(solution)/shard_map/ppermute | solution.py:454
  102.0 5.9 %collective-permute-start.28 = (bf16[2,64,512]{2,1,0:T(8,128)(2,1)S(1)}, bf16[2,64,512]{2,1,0:T(8,128)(2,1)S(1)}, u32[]{:S(2)}, u32[]{:S(2)}) collective-permute-start(bf16[2,64,512]{2,1,0:T(8,128)(2,1)S(1)} %bitcast.26), channel_id=1, source_target_pairs={{4,0},{8,4},{12,8},{16,12},{20,16},{24,20},{28,24},{5,1},{9,5},{13... | collective-permute-start | bytes 393224 | tf_op jit(solution)/shard_map/ppermute | solution.py:454
  107.9 7.5 %collective-permute-start.29 = (bf16[12,2,512]{2,1,0:T(2,128)(2,1)S(1)}, bf16[12,2,512]{2,1,0:T(2,128)(2,1)S(1)}, u32[]{:S(2)}, u32[]{:S(2)}) collective-permute-start(bf16[12,2,512]{2,1,0:T(2,128)(2,1)S(1)} %pad_maximum_fusion), channel_id=1, source_target_pairs={{0,1},{1,2},{2,3},{4,5},{5,6},{6,7},{8,9},{9,10},{10,11},{12,13},{... | collective-permute-start | bytes 73736 | tf_op jit(solution)/shard_map/ppermute | solution.py:454
  113.4 5.1 %collective-permute-start.30 = (bf16[12,2,512]{2,1,0:T(2,128)(2,1)S(1)}, bf16[12,2,512]{2,1,0:T(2,128)(2,1)S(1)}, u32[]{:S(2)}, u32[]{:S(2)}) collective-permute-start(bf16[12,2,512]{2,1,0:T(2,128)(2,1)S(1)} %pad_maximum_fusion.1), channel_id=1, source_target_pairs={{1,0},{2,1},{3,2},{5,4},{6,5},{7,6},{9,8},{10,9},{11,10},{13,12},{... | collective-permute-start | bytes 73736 | tf_op jit(solution)/shard_map/ppermute | solution.py:454
